TPU v7x, 256 devices: a whole 4x4x8 slice. The times are simulated.
256 devices in a mesh: ops: 16 (over x, z_lo, core), sec: 16 (over z_hi, y).
Axes of the slice: x: 4, y: 4, z: 8 (z_hi: 4, z_lo: 2; z = z_hi * 2 + z_lo), core: 2. Of those that a mesh axis runs over, the one named last changes fastest.
Arguments:
- wavefunction: float32 [16, 640, 640], P('sec'), may hold values from -6 to 6
- left_ops: bfloat16 [16, 48, 640, 640], P('sec', 'ops'), may hold values from -0.3125 to 0.3125
- right_ops: bfloat16 [16, 48, 640, 640], P('sec', 'ops'), may hold values from -0.25 to 0.25
- charge_step: int32 [16, 48], P('sec', 'ops'), may hold values from -1 to 1
- sector_sizes: int32 [16], replicated, may hold values from 320 to 640
Outputs:
- cheb_prev: float32 [16, 640, 640], P('sec', 'ops')
- cheb_last: float32 [16, 640, 640], P('sec', 'ops')
Inputs may be any that keep to these rules, and one draw needn't show every extreme that they name: Operator pair p of sector t reads sector t + charge_step[t, p].
All inputs are finite; a program needn't handle non-finite values.
Results may differ from a plain program's by a relative error of at most 0.0076.
Values may be sent and summed in bfloat16 or wider, within the bound.
No kernel may reach another device: no remote copies, remote signals or barrier semaphores. Data moves between devices by JAX's collectives and lax.ppermute only.
A program may use at most 64 MiB of HBM per device.

v0:
```python
import functools
import math

import jax
import jax.numpy as jnp
from jax import lax
from jax.experimental import pallas as pl
from jax.experimental.pallas import tpu as pltpu
from jax.sharding import PartitionSpec as P


STEPS = 2
AXES = ("ops", "sec")
VMEM = pl.BlockSpec(memory_space=pltpu.VMEM)
SMEM = pl.BlockSpec(memory_space=pltpu.SMEM)
ANY = pl.BlockSpec(memory_space=pl.ANY)
HBM = pl.BlockSpec(memory_space=pltpu.HBM)
MIB = 2**20


def swaps(ops_count, sec_count, partner):
    found = []
    for o in range(ops_count):
        for s in range(sec_count):
            to_o, to_s = partner(o, s)
            if 0 <= to_s < sec_count:
                found.append((o * sec_count + s, to_o * sec_count + to_s))
    return found


def in_hbm(array):
    return pltpu.with_memory_space_constraint(array, pltpu.HBM)


def live(size, first, rows, width):
    row = lax.broadcasted_iota(jnp.int32, (rows, width), 0) + first
    col = lax.broadcasted_iota(jnp.int32, (rows, width), 1)
    return jnp.where((row < size) & (col < size), 1.0, 0.0)


def first_kernel(sizes_ref, wave_ref, half_ref, slice_ref, half_buf, slice_buf, sizes_buf, sems):
    share, width = slice_ref.shape
    half = width // 2
    ops_at, sec_at = lax.axis_index("ops"), lax.axis_index("sec")
    half_row = pl.multiple_of(half * lax.rem(ops_at, 2), 8)
    slice_row = pl.multiple_of(half_row + share * (ops_at // 2), 8)
    copies = [
        pltpu.make_async_copy(sizes_ref, sizes_buf, sems.at[0]),
        pltpu.make_async_copy(wave_ref.at[pl.ds(slice_row, share), :], slice_buf, sems.at[1]),
        pltpu.make_async_copy(wave_ref.at[pl.ds(half_row, half), :], half_buf, sems.at[2]),
    ]
    for copy in copies:
        copy.start()
    for copy in copies[:2]:
        copy.wait()
    size = sizes_buf[sec_at]
    slice_ref[...] = (slice_buf[...] * live(size, slice_row, share, width)).astype(jnp.bfloat16)
    copies[2].wait()
    half_ref[...] = (half_buf[...] * live(size, half_row, half, width)).astype(jnp.bfloat16)


def prepare_first(sizes, wave, share):
    width = wave.shape[0]
    half = width // 2
    return pl.pallas_call(
        first_kernel,
        in_specs=[HBM, HBM],
        out_specs=[VMEM, VMEM],
        out_shape=[
            jax.ShapeDtypeStruct((half, width), jnp.bfloat16),
            jax.ShapeDtypeStruct((share, width), jnp.bfloat16),
        ],
        scratch_shapes=[
            pltpu.VMEM((half, width), jnp.float32),
            pltpu.VMEM((share, width), jnp.float32),
            pltpu.SMEM(sizes.shape, jnp.int32),
            pltpu.SemaphoreType.DMA((3,)),
        ],
        compiler_params=pltpu.CompilerParams(vmem_limit_bytes=4 * MIB),
        cost_estimate=pl.CostEstimate(flops=width**2, bytes_accessed=3 * width**2, transcendentals=0),
    )(in_hbm(sizes), in_hbm(wave))


def rest_kernel(norm_scale, sizes_ref, wave_ref, own_ref, start_ref, mask_ref):
    share, width = start_ref.shape
    size = sizes_ref[lax.axis_index("sec")]
    first = pl.multiple_of(share * lax.axis_index("ops"), 8)
    own_ref[...] = (wave_ref[...] * live(size, 0, width, width)).astype(jnp.bfloat16)
    mask = live(size, first, share, width)
    start_ref[...] = wave_ref[pl.ds(first, share), :] * mask
    mask_ref[...] = mask * norm_scale


def prepare_rest(sizes, wave, share, norm_scale):
    width = wave.shape[0]
    return pl.pallas_call(
        functools.partial(rest_kernel, norm_scale),
        in_specs=[SMEM, VMEM],
        out_specs=[VMEM] * 3,
        out_shape=[
            jax.ShapeDtypeStruct((width, width), jnp.bfloat16),
            jax.ShapeDtypeStruct((share, width), jnp.float32),
            jax.ShapeDtypeStruct((share, width), jnp.float32),
        ],
        compiler_params=pltpu.CompilerParams(vmem_limit_bytes=8 * MIB),
        cost_estimate=pl.CostEstimate(flops=width**2, bytes_accessed=6 * width**2, transcendentals=0),
    )(sizes, wave)


def apply_kernel(n_whole, charge_ref, *refs):
    wholes, (near_ref, far_ref, left_hbm, right_hbm, mine_ref, other_ref) = refs[:n_whole], refs[n_whole : n_whole + 6]
    field_ref, half_ref, total_ref, left_ref, right_ref, left_sems, right_sems, whole_sems = refs[n_whole + 6 :]
    count, width, _ = left_ref.shape
    blocks, share, _ = mine_ref.shape
    half = width // 2
    ops_at, sec_at = lax.axis_index("ops"), lax.axis_index("sec")
    core, parity = lax.rem(ops_at, 2), lax.rem(sec_at, 2)

    copies = []
    for k, ref in enumerate(wholes):
        if k == 0:
            target = field_ref.at[0]
        else:
            owner = core if k == 1 else 1 - core
            target = field_ref.at[1, pl.ds(pl.multiple_of(half * owner, 16), half), :]
        copies.append(pltpu.make_async_copy(ref, target, whole_sems.at[k]))
    lefts = [pltpu.make_async_copy(left_hbm.at[p], left_ref.at[p], left_sems.at[p]) for p in range(count)]
    rights = [pltpu.make_async_copy(right_hbm.at[p], right_ref.at[p], right_sems.at[p]) for p in range(count)]
    for copy in copies + lefts + rights:
        copy.start()

    for c in range(2):

        @pl.when(core == c)
        def _():
            for part, owner in ((near_ref, c), (far_ref, 1 - c)):
                for block in range(blocks):
                    if n_whole:
                        row = owner * half + block * share
                        field_ref[2, row : row + share, :] = part[block]
                    else:
                        row = (2 * block + owner) * share
                        for slot in range(3):
                            field_ref[slot, row : row + share, :] = part[block, slot]

    for copy in copies:
        copy.wait()
    for pair in range(count):
        charge = charge_ref[0, pair]
        slot = jnp.where(charge == 0, 0, jnp.where((charge > 0) == (parity == 0), 1, 2))
        lefts[pair].wait()
        half_ref[:, width * pair : width * (pair + 1)] = jnp.dot(
            left_ref[pair], field_ref[slot], preferred_element_type=jnp.float32
        ).astype(jnp.bfloat16)
    for copy in rights:
        copy.wait()
    total_ref[...] = sum(
        lax.dot_general(
            half_ref[:, width * pair : width * (pair + 1)],
            right_ref[pair],
            (((1,), (1,)), ((), ())),
            preferred_element_type=jnp.float32,
        )
        for pair in range(count)
    )
    for c in range(2):

        @pl.when(core == c)
        def _():
            for block in range(blocks):
                row = (2 * block + c) * share
                mine_ref[block] = total_ref[row : row + share, :]
                row = (2 * block + 1 - c) * share
                other_ref[block] = total_ref[row : row + share, :].astype(jnp.bfloat16)


def apply_pairs(charge, wholes, near, far, left, right, share):
    count, width, _ = left.shape
    blocks = width // share // 2
    return pl.pallas_call(
        functools.partial(apply_kernel, len(wholes)),
        in_specs=[SMEM] + [ANY] * len(wholes) + [VMEM, VMEM, HBM, HBM],
        out_specs=[VMEM, VMEM],
        out_shape=[
            jax.ShapeDtypeStruct((blocks, share, width), jnp.float32),
            jax.ShapeDtypeStruct((blocks, share, width), jnp.bfloat16),
        ],
        scratch_shapes=[
            pltpu.VMEM((3, width, width), jnp.bfloat16),
            pltpu.VMEM((width, count * width), jnp.bfloat16),
            pltpu.VMEM((width, width), jnp.float32),
            pltpu.VMEM((count, width, width), jnp.bfloat16),
            pltpu.VMEM((count, width, width), jnp.bfloat16),
            pltpu.SemaphoreType.DMA((count,)),
            pltpu.SemaphoreType.DMA((count,)),
            pltpu.SemaphoreType.DMA((3,)),
        ],
        compiler_params=pltpu.CompilerParams(vmem_limit_bytes=24 * MIB),
        cost_estimate=pl.CostEstimate(
            flops=4 * count * width**3, bytes_accessed=4 * count * width**2, transcendentals=0
        ),
    )(charge, *wholes, near, far, in_hbm(left), in_hbm(right))


def on_device(wavefunction, left_ops, right_ops, charge_step, sector_sizes):
    ops_count, sec_count = lax.axis_size("ops"), lax.axis_size("sec")
    chips = ops_count // 2
    width = wavefunction.shape[1]
    share = width // ops_count
    norm_scale = 1.0 / math.sqrt(left_ops.shape[1] * ops_count)
    partner_core = swaps(ops_count, sec_count, lambda o, s: (o ^ 1, s))
    even = swaps(ops_count, sec_count, lambda o, s: (o, s ^ 1))
    odd = swaps(ops_count, sec_count, lambda o, s: (o, s + 1 if s % 2 else s - 1))
    same_core = [[o for o in range(ops_count) if o % 2 == c] for c in range(2)]

    def send(block, where):
        return lax.ppermute(block, AXES, where)

    def exchange(tiles):
        return lax.all_to_all(tiles, "ops", 0, 0, axis_index_groups=same_core, tiled=True)

    def spread(rows):
        return exchange(jnp.broadcast_to(rows[None], (chips, *rows.shape)))

    half, first = prepare_first(sector_sizes, wavefunction[0], share)
    own, start_rows, scaled_mask = prepare_rest(sector_sizes, wavefunction[0], share, norm_scale)
    even_near = send(half, even)
    odd_rows = send(first, odd)
    near = spread(odd_rows)
    even_far = send(even_near, partner_core)
    far = send(near, partner_core)
    wholes = [own, even_near, even_far]

    outputs = [start_rows]
    for iteration in range(STEPS):
        mine, other = apply_pairs(charge_step, wholes, near, far, left_ops[0], right_ops[0], share)
        chip_sum = (mine + send(other, partner_core).astype(jnp.float32)).astype(jnp.bfloat16)
        applied = exchange(chip_sum).astype(jnp.float32).sum(axis=0) * scaled_mask
        updated = applied if iteration == 0 else 2.0 * applied - outputs[-2]
        outputs.append(updated)
        if iteration + 1 < STEPS:
            rows = updated.astype(jnp.bfloat16)
            even_rows = send(rows, even)
            three = jnp.stack([rows, even_rows, send(rows, odd)])
            near = spread(three)
            far = send(near, partner_core)
            wholes = []
    return (outputs[-2][None], outputs[-1][None])


def solution(mesh):
    in_specs = (
        P("sec", None, None),
        P("sec", "ops", None, None),
        P("sec", "ops", None, None),
        P("sec", "ops"),
        P(),
    )
    out_specs = (P("sec", "ops", None), P("sec", "ops", None))
    return jax.shard_map(
        on_device, mesh=mesh, in_specs=in_specs, out_specs=out_specs, check_vma=False
    )
```

profile of v0, /device:TPU:128, one launch (start us, length us, event | category | flops | bytes accessed | tf_op | source)
XLA Modules:
  0.0 109.3 jit_solution(8764242898486128259)
XLA Ops:
  0.6 1.4 %shard_map.69 = (bf16[320,640]{1,0:T(8,128)(2,1)S(1)}, bf16[40,640]{1,0:T(8,128)(2,1)S(1)}) custom-call(s32[16]{0:T(128)} %sizes_ref.3, f32[640,640]{1,0:T(8,128)} %bitcast.10), custom_call_target="tpu_custom_call" | custom-call | flops 409600 | bytes 1228800 | tf_op jit(solution)/shard_map/pallas_call | solution.py:65
  2.1 4.0 %collective-permute-start.2 = (bf16[40,640]{1,0:T(8,128)(2,1)S(1)}, bf16[40,640]{1,0:T(8,128)(2,1)S(1)}, u32[]{:S(2)}, u32[]{:S(2)}) collective-permute-start(bf16[40,640]{1,0:T(8,128)(2,1)S(1)} %get-tuple-element.13), channel_id=1, source_target_pairs={{1,2},{2,1},{3,4},{4,3},{5,6},{6,5},{7,8},{8,7},{9,10},{10,9},{11,... | collective-permute-start | bytes 153608 | tf_op jit(solution)/shard_map/ppermute | solution.py:217
  6.1 6.3 %collective-permute-done.2 = bf16[40,640]{1,0:T(8,128)(2,1)S(1)} collective-permute-done((bf16[40,640]{1,0:T(8,128)(2,1)S(1)}, bf16[40,640]{1,0:T(8,128)(2,1)S(1)}, u32[]{:S(2)}, u32[]{:S(2)}) %collective-permute-start.2) | collective-permute-done | bytes 51232 | tf_op jit(solution)/shard_map/ppermute | solution.py:217
  12.4 0.8 broadcast_in_dim.8
  13.2 5.2 %all-to-all-start = ((bf16[8,40,640]{2,1,0:T(8,128)(2,1)}), bf16[8,40,640]{2,1,0:T(8,128)(2,1)S(1)}, u32[]{:S(2)}, u32[]{:S(2)}) async-start(bf16[8,40,640]{2,1,0:T(8,128)(2,1)} %broadcast_in_dim.8), calls=%async_computation | async-start | bytes 819200 | tf_op jit(solution)/shard_map/all_to_all | solution.py:220
  18.4 9.2 %collective-permute-done.refs_1_ = bf16[320,640]{1,0:T(8,128)(2,1)S(1)} collective-permute-done((bf16[320,640]{1,0:T(8,128)(2,1)S(1)}, bf16[320,640]{1,0:T(8,128)(2,1)S(1)}, u32[]{:S(2)}, u32[]{:S(2)}) %collective-permute-start) | collective-permute-done | bytes 409632 | tf_op jit(solution)/shard_map/ppermute | solution.py:217
  27.7 0.5 collective-permute-start.3
  28.2 0.7 shard_map.68
  28.9 0.5 collective-permute-done.1.refs_2_
  29.4 0.6 collective-permute-done.3.refs_4_
  30.0 7.9 %shard_map.70 = (f32[8,40,640]{2,1,0:T(8,128)S(1)}, bf16[8,40,640]{2,1,0:T(8,128)(2,1)S(1)}) custom-call(s32[1,3]{1,0:T(1,128)S(1)} %copy-done.2, bf16[640,640]{1,0:T(8,128)(2,1)S(1)} %get-tuple-element.11.refs_0_, bf16[320,640]{1,0:T(8,128)(2,1)S(1)} %collective-permute-done.refs_1_, bf16[320,640]{1,0:T(8,128)(2,1)S(1)} %collective-permute-done.1.refs_2_, ...), custom_call_target="tpu_custom_call" | custom-call | flops 3145728000 | bytes 4915200 | tf_op jit(solution)/shard_map/pallas_call | solution.py:180
  38.0 0.3 collective-permute-start.4
  38.2 1.6 %collective-permute-done.4 = bf16[8,40,640]{2,1,0:T(8,128)(2,1)S(1)} collective-permute-done((bf16[8,40,640]{2,1,0:T(8,128)(2,1)S(1)}, bf16[8,40,640]{2,1,0:T(8,128)(2,1)S(1)}, u32[]{:S(2)}, u32[]{:S(2)}) %collective-permute-start.4) | collective-permute-done | bytes 409632 | tf_op jit(solution)/shard_map/ppermute | solution.py:217
  39.9 14.5 %all_to_all.20 = bf16[8,40,640]{2,1,0:T(8,128)(2,1)S(1)} all-to-all(bf16[8,40,640]{2,1,0:T(8,128)(2,1)S(1)} %add_convert_fusion.1), channel_id=1, replica_groups={{0,32,64,96,128,160,192,224},{16,48,80,112,144,176,208,240},{1,33,65,97..., dimensions={0} | all-to-all | bytes 819200 | tf_op jit(solution)/shard_map/all_to_all | solution.py:220
  54.4 0.7 multiply_convert_fusion
  55.1 5.0 %collective-permute-start.6 = (bf16[40,640]{1,0:T(8,128)(2,1)S(1)}, bf16[40,640]{1,0:T(8,128)(2,1)S(1)}, u32[]{:S(2)}, u32[]{:S(2)}) collective-permute-start(bf16[40,640]{1,0:T(8,128)(2,1)S(1)} %get-tuple-element.20), channel_id=1, source_target_pairs={{1,2},{2,1},{3,4},{4,3},{5,6},{6,5},{7,8},{8,7},{9,10},{10,9},{11,... | collective-permute-start | bytes 153608 | tf_op jit(solution)/shard_map/ppermute | solution.py:217
  60.2 5.1 %collective-permute-done.6 = bf16[40,640]{1,0:T(8,128)(2,1)S(1)} collective-permute-done((bf16[40,640]{1,0:T(8,128)(2,1)S(1)}, bf16[40,640]{1,0:T(8,128)(2,1)S(1)}, u32[]{:S(2)}, u32[]{:S(2)}) %collective-permute-start.6) | collective-permute-done | bytes 51232 | tf_op jit(solution)/shard_map/ppermute | solution.py:217
  65.4 19.0 %all_to_all.21.refs_0_ = bf16[8,3,40,640]{3,2,1,0:T(8,128)(2,1)S(1)} all-to-all(bf16[8,3,40,640]{3,2,1,0:T(8,128)(2,1)S(1)} %broadcast_in_dim.20), channel_id=1, replica_groups={{0,32,64,96,128,160,192,224},{16,48,80,112,144,176,208,240},{1,33,65,97..., dimensions={0} | all-to-all | bytes 2457600 | tf_op jit(solution)/shard_map/all_to_all | solution.py:220
  84.4 2.9 %collective-permute-done.7.refs_1_ = bf16[8,3,40,640]{3,2,1,0:T(8,128)(2,1)S(1)} collective-permute-done((bf16[8,3,40,640]{3,2,1,0:T(8,128)(2,1)S(1)}, bf16[8,3,40,640]{3,2,1,0:T(8,128)(2,1)S(1)}, u32[]{:S(2)}, u32[]{:S(2)}) %collective-permute-start.7) | collective-permute-done | bytes 1228832 | tf_op jit(solution)/shard_map/ppermute | solution.py:217
  87.3 7.4 %shard_map.71 = (f32[8,40,640]{2,1,0:T(8,128)S(1)}, bf16[8,40,640]{2,1,0:T(8,128)(2,1)S(1)}) custom-call(s32[1,3]{1,0:T(1,128)S(1)} %copy-done.2, bf16[8,3,40,640]{3,2,1,0:T(8,128)(2,1)S(1)} %all_to_all.21.refs_0_, bf16[8,3,40,640]{3,2,1,0:T(8,128)(2,1)S(1)} %collective-permute-done.7.refs_1_, bf16[3,640,640]{2,1,0:T(8,128)(2,1)} %bitcast.16, ...), custom_call_target="tpu_custom_call" | custom-call | flops 3145728000 | bytes 4915200 | tf_op jit(solution)/shard_map/pallas_call | solution.py:180
  94.8 0.2 collective-permute-start.8
  95.0 1.6 %collective-permute-done.8 = bf16[8,40,640]{2,1,0:T(8,128)(2,1)S(1)} collective-permute-done((bf16[8,40,640]{2,1,0:T(8,128)(2,1)S(1)}, bf16[8,40,640]{2,1,0:T(8,128)(2,1)S(1)}, u32[]{:S(2)}, u32[]{:S(2)}) %collective-permute-start.8) | collective-permute-done | bytes 409632 | tf_op jit(solution)/shard_map/ppermute | solution.py:217
  96.7 11.9 %all_to_all.22 = bf16[8,40,640]{2,1,0:T(8,128)(2,1)S(1)} all-to-all(bf16[8,40,640]{2,1,0:T(8,128)(2,1)S(1)} %add_convert_fusion), channel_id=1, replica_groups={{0,32,64,96,128,160,192,224},{16,48,80,112,144,176,208,240},{1,33,65,97..., dimensions={0} | all-to-all | bytes 819200 | tf_op jit(solution)/shard_map/all_to_all | solution.py:220
  108.7 0.7 subtract_bitcast_fusion
  (18 shorter events, 0.5 us)
Async XLA Ops:
  0.6 27.6 %copy-start.1 = (s32[16]{0:T(128)S(1)}, s32[16]{0:T(128)}, u32[]{:S(2)}) copy-start(s32[16]{0:T(128)} %sizes_ref.3) | copy-start | bytes 196
  0.6 27.6 %copy-start = (f32[1,640,640]{2,1,0:T(8,128)S(1)}, f32[1,640,640]{2,1,0:T(8,128)}, u32[]{:S(2)}) copy-start(f32[1,640,640]{2,1,0:T(8,128)} %param.5) | copy-start | bytes 4915204
  2.1 27.9 %copy-start.2 = (s32[1,3]{1,0:T(1,128)S(1)}, s32[1,3]{1,0:T(1,128)}, u32[]{:S(2)}) copy-start(s32[1,3]{1,0:T(1,128)} %charge_ref.3) | copy-start | bytes 40
  2.1 10.3 %collective-permute-start.2 = (bf16[40,640]{1,0:T(8,128)(2,1)S(1)}, bf16[40,640]{1,0:T(8,128)(2,1)S(1)}, u32[]{:S(2)}, u32[]{:S(2)}) collective-permute-start(bf16[40,640]{1,0:T(8,128)(2,1)S(1)} %get-tuple-element.13), channel_id=1, source_target_pairs={{1,2},{2,1},{3,4},{4,3},{5,6},{6,5},{7,8},{8,7},{9,10},{10,9},{11,... | collective-permute-start | bytes 153608 | tf_op jit(solution)/shard_map/ppermute | solution.py:217
  13.2 14.5 %all-to-all-start = ((bf16[8,40,640]{2,1,0:T(8,128)(2,1)}), bf16[8,40,640]{2,1,0:T(8,128)(2,1)S(1)}, u32[]{:S(2)}, u32[]{:S(2)}) async-start(bf16[8,40,640]{2,1,0:T(8,128)(2,1)} %broadcast_in_dim.8), calls=%async_computation | async-start | bytes 819200 | tf_op jit(solution)/shard_map/all_to_all | solution.py:220
  18.4 9.3 %collective-permute-start = (bf16[320,640]{1,0:T(8,128)(2,1)S(1)}, bf16[320,640]{1,0:T(8,128)(2,1)S(1)}, u32[]{:S(2)}, u32[]{:S(2)}) collective-permute-start(bf16[320,640]{1,0:T(8,128)(2,1)S(1)} %get-tuple-element.12), channel_id=1, source_target_pairs={{0,1},{1,0},{2,3},{3,2},{4,5},{5,4},{6,7},{7,6},{8,9},{9,8},{10,11... | collective-permute-start | bytes 1228808 | tf_op jit(solution)/shard_map/ppermute | solution.py:217
  27.7 1.7 %collective-permute-start.1 = (bf16[320,640]{1,0:T(8,128)(2,1)S(1)}, bf16[320,640]{1,0:T(8,128)(2,1)S(1)}, u32[]{:S(2)}, u32[]{:S(2)}) collective-permute-start(bf16[320,640]{1,0:T(8,128)(2,1)S(1)} %collective-permute-done.refs_1_), channel_id=1, source_target_pairs={{0,16},{1,17},{2,18},{3,19},{4,20},{5,21},{6,22},{7,23},{8,24},{9,... | collective-permute-start | bytes 1228808 | tf_op jit(solution)/shard_map/ppermute | solution.py:217
  27.7 2.3 %collective-permute-start.3 = (bf16[8,40,640]{2,1,0:T(8,128)(2,1)S(1)}, bf16[8,40,640]{2,1,0:T(8,128)(2,1)S(1)}, u32[]{:S(2)}, u32[]{:S(2)}) collective-permute-start(bf16[8,40,640]{2,1,0:T(8,128)(2,1)S(1)} %all-to-all-done.refs_3_), channel_id=1, source_target_pairs={{0,16},{1,17},{2,18},{3,19},{4,20},{5,21},{6,22},{7,23},{8,24},{9,... | collective-permute-start | bytes 1228808 | tf_op jit(solution)/shard_map/ppermute | solution.py:217
  38.0 1.8 %collective-permute-start.4 = (bf16[8,40,640]{2,1,0:T(8,128)(2,1)S(1)}, bf16[8,40,640]{2,1,0:T(8,128)(2,1)S(1)}, u32[]{:S(2)}, u32[]{:S(2)}) collective-permute-start(bf16[8,40,640]{2,1,0:T(8,128)(2,1)S(1)} %get-tuple-element.15), channel_id=1, source_target_pairs={{0,16},{1,17},{2,18},{3,19},{4,20},{5,21},{6,22},{7,23},{8,24},{9,... | collective-permute-start | bytes 1228808 | tf_op jit(solution)/shard_map/ppermute | solution.py:217
  55.1 10.2 %collective-permute-start.6 = (bf16[40,640]{1,0:T(8,128)(2,1)S(1)}, bf16[40,640]{1,0:T(8,128)(2,1)S(1)}, u32[]{:S(2)}, u32[]{:S(2)}) collective-permute-start(bf16[40,640]{1,0:T(8,128)(2,1)S(1)} %get-tuple-element.20), channel_id=1, source_target_pairs={{1,2},{2,1},{3,4},{4,3},{5,6},{6,5},{7,8},{8,7},{9,10},{10,9},{11,... | collective-permute-start | bytes 153608 | tf_op jit(solution)/shard_map/ppermute | solution.py:217
  60.1 5.2 %collective-permute-start.5 = (bf16[40,640]{1,0:T(8,128)(2,1)S(1)}, bf16[40,640]{1,0:T(8,128)(2,1)S(1)}, u32[]{:S(2)}, u32[]{:S(2)}) collective-permute-start(bf16[40,640]{1,0:T(8,128)(2,1)S(1)} %get-tuple-element.20), channel_id=1, source_target_pairs={{0,1},{1,0},{2,3},{3,2},{4,5},{5,4},{6,7},{7,6},{8,9},{9,8},{10,11... | collective-permute-start | bytes 153608 | tf_op jit(solution)/shard_map/ppermute | solution.py:217
  84.4 2.9 %collective-permute-start.7 = (bf16[8,3,40,640]{3,2,1,0:T(8,128)(2,1)S(1)}, bf16[8,3,40,640]{3,2,1,0:T(8,128)(2,1)S(1)}, u32[]{:S(2)}, u32[]{:S(2)}) collective-permute-start(bf16[8,3,40,640]{3,2,1,0:T(8,128)(2,1)S(1)} %all_to_all.21.refs_0_), channel_id=1, source_target_pairs={{0,16},{1,17},{2,18},{3,19},{4,20},{5,21},{6,22},{7,23},{8,24},{9,... | collective-permute-start | bytes 3686408 | tf_op jit(solution)/shard_map/ppermute | solution.py:217
  94.8 1.8 %collective-permute-start.8 = (bf16[8,40,640]{2,1,0:T(8,128)(2,1)S(1)}, bf16[8,40,640]{2,1,0:T(8,128)(2,1)S(1)}, u32[]{:S(2)}, u32[]{:S(2)}) collective-permute-start(bf16[8,40,640]{2,1,0:T(8,128)(2,1)S(1)} %get-tuple-element.18), channel_id=1, source_target_pairs={{0,16},{1,17},{2,18},{3,19},{4,20},{5,21},{6,22},{7,23},{8,24},{9,... | collective-permute-start | bytes 1228808 | tf_op jit(solution)/shard_map/ppermute | solution.py:217
where the time goes:
time: 110 us; the launch traced here: 109 us
  blocking collectives  45.4 us (41%)
  waiting for transfers between devices  27.9 us (25%)
  Pallas kernels  17.5 us (16%)
  starting transfers between devices  15.3 us (14%)
  other arithmetic  1.64 us (1%)
    all_to_all x3, blocking collectives, exchange(): lax.all_to_all(tiles, 'ops', 0, 0, axis_index_groups=same_core, tiled=True)  45.4 us
    ppermute x9, waiting for transfers between devices, send(): return lax.ppermute(block, AXES, where)  27.9 us
    pallas_call x2, Pallas kernels, apply_pairs(): pl.pallas_call(functools.partial(apply_kernel, len(wholes)), in_specs=[SM...  15.3 us
    ppermute x9, starting transfers between devices, send(): return lax.ppermute(block, AXES, where)  10.1 us
    all_to_all x1, starting transfers between devices, exchange(): lax.all_to_all(tiles, 'ops', 0, 0, axis_index_groups=same_core, tiled=True)  5.2 us
  transfers between devices with their start and end apart: 10, of which 8 were waited for; matrix products, arithmetic and copies ran while one was open for 0% of the time, Pallas kernels for 1%

commit v1 on v0

v1 whole, which is shorter than its diff:
```python
import functools
import math

import jax
import jax.numpy as jnp
from jax import lax
from jax.experimental import pallas as pl
from jax.experimental.pallas import tpu as pltpu
from jax.sharding import PartitionSpec as P


STEPS = 2
AXES = ("ops", "sec")
VMEM = pl.BlockSpec(memory_space=pltpu.VMEM)
SMEM = pl.BlockSpec(memory_space=pltpu.SMEM)
ANY = pl.BlockSpec(memory_space=pl.ANY)
HBM = pl.BlockSpec(memory_space=pltpu.HBM)
MIB = 2**20


def swaps(ops_count, sec_count, partner):
    found = []
    for o in range(ops_count):
        for s in range(sec_count):
            to_o, to_s = partner(o, s)
            if 0 <= to_s < sec_count:
                found.append((o * sec_count + s, to_o * sec_count + to_s))
    return found


def in_hbm(array):
    return pltpu.with_memory_space_constraint(array, pltpu.HBM)


def live(size, first, rows, width):
    row = lax.broadcasted_iota(jnp.int32, (rows, width), 0) + first
    col = lax.broadcasted_iota(jnp.int32, (rows, width), 1)
    return jnp.where((row < size) & (col < size), 1.0, 0.0)


def cut_kernel(first_row, sizes_ref, wave_ref, out_ref, wave_buf, sizes_buf, sems):
    rows, width = out_ref.shape
    first = pl.multiple_of(first_row(lax.axis_index("ops")), 8)
    copies = [
        pltpu.make_async_copy(sizes_ref, sizes_buf, sems.at[0]),
        pltpu.make_async_copy(wave_ref.at[pl.ds(first, rows), :], wave_buf, sems.at[1]),
    ]
    for copy in copies:
        copy.start()
    for copy in copies:
        copy.wait()
    size = sizes_buf[lax.axis_index("sec")]
    out_ref[...] = (wave_buf[...] * live(size, first, rows, width)).astype(jnp.bfloat16)


def masked_rows(sizes, wave, rows, first_row):
    width = wave.shape[0]
    return pl.pallas_call(
        functools.partial(cut_kernel, first_row),
        in_specs=[HBM, HBM],
        out_specs=VMEM,
        out_shape=jax.ShapeDtypeStruct((rows, width), jnp.bfloat16),
        scratch_shapes=[
            pltpu.VMEM((rows, width), jnp.float32),
            pltpu.SMEM(sizes.shape, jnp.int32),
            pltpu.SemaphoreType.DMA((2,)),
        ],
        compiler_params=pltpu.CompilerParams(vmem_limit_bytes=4 * MIB),
        cost_estimate=pl.CostEstimate(flops=rows * width, bytes_accessed=6 * rows * width, transcendentals=0),
    )(in_hbm(sizes), in_hbm(wave))


def rest_kernel(norm_scale, sizes_ref, wave_ref, left_hbm, own_hbm, start_ref, mask_ref, left_ref, own_buf, sizes_buf, sems, own_sem, sizes_sem):
    share, width = start_ref.shape
    count, owners, blocks = left_ref.shape[0], 2, width // share // 2
    copies = []
    for pair in range(count):
        for owner in range(owners):
            for block in range(blocks):
                copies.append(
                    pltpu.make_async_copy(
                        left_hbm.at[pair, pl.ds((2 * block + owner) * share, share), :],
                        left_ref.at[pair, pl.ds((owner * blocks + block) * share, share), :],
                        sems.at[(pair * owners + owner) * blocks + block],
                    )
                )
    sizes_copy = pltpu.make_async_copy(sizes_ref, sizes_buf, sizes_sem)
    for copy in [sizes_copy] + copies:
        copy.start()
    sizes_copy.wait()
    size = sizes_buf[lax.axis_index("sec")]
    first = pl.multiple_of(share * lax.axis_index("ops"), 8)
    own_buf[...] = (wave_ref[...] * live(size, 0, width, width)).astype(jnp.bfloat16)
    own_copy = pltpu.make_async_copy(own_buf, own_hbm, own_sem)
    own_copy.start()
    mask = live(size, first, share, width)
    start_ref[...] = wave_ref[pl.ds(first, share), :] * mask
    mask_ref[...] = mask * norm_scale
    for copy in copies + [own_copy]:
        copy.wait()


def prepare_rest(sizes, wave, left, share, norm_scale):
    width = wave.shape[0]
    return pl.pallas_call(
        functools.partial(rest_kernel, norm_scale),
        in_specs=[HBM, VMEM, HBM],
        out_specs=[HBM] + [VMEM] * 3,
        out_shape=[
            pltpu.HBM((width, width), jnp.bfloat16),
            jax.ShapeDtypeStruct((share, width), jnp.float32),
            jax.ShapeDtypeStruct((share, width), jnp.float32),
            jax.ShapeDtypeStruct(left.shape, left.dtype),
        ],
        scratch_shapes=[
            pltpu.VMEM((width, width), jnp.bfloat16),
            pltpu.SMEM(sizes.shape, jnp.int32),
            pltpu.SemaphoreType.DMA((left.shape[0] * width // share,)),
            pltpu.SemaphoreType.DMA,
            pltpu.SemaphoreType.DMA,
        ],
        compiler_params=pltpu.CompilerParams(vmem_limit_bytes=12 * MIB),
        cost_estimate=pl.CostEstimate(flops=width**2, bytes_accessed=18 * width**2, transcendentals=0),
    )(in_hbm(sizes), wave, in_hbm(left))


def products(charge_ref, field_ref, left_ref, right_ref, half_ref, owner, before_right):
    count, width, _ = left_ref.shape
    rows = width // 2
    parity = lax.rem(lax.axis_index("sec"), 2)
    first = pl.multiple_of(rows * owner, 16)
    for pair in range(count):
        charge = charge_ref[0, pair]
        slot = jnp.where(charge == 0, 0, jnp.where((charge > 0) == (parity == 0), 1, 2))
        half_ref[:, width * pair : width * (pair + 1)] = jnp.dot(
            left_ref[pair, pl.ds(first, rows), :], field_ref[slot], preferred_element_type=jnp.float32
        ).astype(jnp.bfloat16)
    before_right()
    return sum(
        lax.dot_general(
            half_ref[:, width * pair : width * (pair + 1)],
            right_ref[pair],
            (((1,), (1,)), ((), ())),
            preferred_element_type=jnp.float32,
        )
        for pair in range(count)
    )


def other_kernel(n_whole, charge_ref, *refs):
    wholes, (near_ref, far_ref, left_ref, right_hbm, other_ref, field_ref, right_ref) = refs[:n_whole], refs[n_whole : n_whole + 7]
    half_ref, right_sem, whole_sems = refs[n_whole + 7 :]
    width = field_ref.shape[1]
    half = width // 2
    core = lax.rem(lax.axis_index("ops"), 2)

    copies = []
    for k, ref in enumerate(wholes):
        if k == 0:
            target = field_ref.at[0]
        else:
            owner = core if k == 1 else 1 - core
            target = field_ref.at[1, pl.ds(pl.multiple_of(half * owner, 16), half), :]
        copies.append(pltpu.make_async_copy(ref, target, whole_sems.at[k]))
    right_copy = pltpu.make_async_copy(right_hbm, right_ref, right_sem)
    for copy in copies or [right_copy]:
        copy.start()

    blocks = near_ref.shape[0]
    share = half // blocks
    for c in range(2):

        @pl.when(core == c)
        def _():
            for part, owner in ((near_ref, c), (far_ref, 1 - c)):
                for block in range(blocks):
                    if n_whole:
                        row = owner * half + block * share
                        field_ref[2, row : row + share, :] = part[block]
                    else:
                        row = (2 * block + owner) * share
                        for slot in range(3):
                            field_ref[slot, row : row + share, :] = part[block, slot]

    for copy in copies:
        copy.wait()
    if copies:
        right_copy.start()
    other_ref[...] = products(
        charge_ref, field_ref, left_ref, right_ref, half_ref, 1 - core, right_copy.wait
    ).astype(jnp.bfloat16)


def mine_kernel(charge_ref, field_ref, left_ref, right_ref, mine_ref, half_ref):
    core = lax.rem(lax.axis_index("ops"), 2)
    mine_ref[...] = products(charge_ref, field_ref, left_ref, right_ref, half_ref, core, lambda: None)


def cost(count, width):
    return pl.CostEstimate(flops=2 * count * width**3, bytes_accessed=4 * count * width**2, transcendentals=0)


def other_rows(charge, wholes, near, far, left, right):
    count, width, _ = left.shape
    return pl.pallas_call(
        functools.partial(other_kernel, len(wholes)),
        in_specs=[SMEM] + [ANY] * len(wholes) + [VMEM, VMEM, VMEM, HBM],
        out_specs=[VMEM] * 3,
        out_shape=[
            jax.ShapeDtypeStruct((width // 2, width), jnp.bfloat16),
            jax.ShapeDtypeStruct((3, width, width), jnp.bfloat16),
            jax.ShapeDtypeStruct(right.shape, right.dtype),
        ],
        scratch_shapes=[
            pltpu.VMEM((width // 2, count * width), jnp.bfloat16),
            pltpu.SemaphoreType.DMA,
            pltpu.SemaphoreType.DMA((3,)),
        ],
        compiler_params=pltpu.CompilerParams(vmem_limit_bytes=20 * MIB),
        cost_estimate=cost(count, width),
    )(charge, *wholes, near, far, left, in_hbm(right))


def mine_rows(charge, field, left, right):
    count, width, _ = left.shape
    return pl.pallas_call(
        mine_kernel,
        in_specs=[SMEM, VMEM, VMEM, VMEM],
        out_specs=VMEM,
        out_shape=jax.ShapeDtypeStruct((width // 2, width), jnp.float32),
        scratch_shapes=[pltpu.VMEM((width // 2, count * width), jnp.bfloat16)],
        compiler_params=pltpu.CompilerParams(vmem_limit_bytes=16 * MIB),
        cost_estimate=cost(count, width),
    )(charge, field, left, right)


def on_device(wavefunction, left_ops, right_ops, charge_step, sector_sizes):
    ops_count, sec_count = lax.axis_size("ops"), lax.axis_size("sec")
    chips = ops_count // 2
    width = wavefunction.shape[1]
    share = width // ops_count
    norm_scale = 1.0 / math.sqrt(left_ops.shape[1] * ops_count)
    partner_core = swaps(ops_count, sec_count, lambda o, s: (o ^ 1, s))
    even = swaps(ops_count, sec_count, lambda o, s: (o, s ^ 1))
    odd = swaps(ops_count, sec_count, lambda o, s: (o, s + 1 if s % 2 else s - 1))
    same_core = [[o for o in range(ops_count) if o % 2 == c] for c in range(2)]

    def send(block, where):
        return lax.ppermute(block, AXES, where)

    def exchange(tiles):
        return lax.all_to_all(tiles, "ops", 0, 0, axis_index_groups=same_core, tiled=True)

    def spread(rows):
        return exchange(jnp.broadcast_to(rows[None], (chips, *rows.shape)))

    wave = wavefunction[0]
    half = width // 2
    first = masked_rows(sector_sizes, wave, share, lambda o: half * lax.rem(o, 2) + share * (o // 2))
    odd_rows = send(first, odd)
    block = masked_rows(sector_sizes, wave, half, lambda o: half * lax.rem(o, 2))
    even_near = send(block, even)
    own, start_rows, scaled_mask, left = prepare_rest(
        sector_sizes, wave, left_ops[0], share, norm_scale
    )
    near = spread(odd_rows)
    near, even_near = lax.optimization_barrier((near, even_near))
    even_far = send(even_near, partner_core)
    far = send(near, partner_core)
    wholes = [in_hbm(own), even_near, even_far]

    outputs = [start_rows]
    for iteration in range(STEPS):
        other, field, right = other_rows(charge_step, wholes, near, far, left, right_ops[0])
        partner_sum = send(other, partner_core)
        mine = mine_rows(charge_step, field, left, right)
        chip_sum = (mine + partner_sum.astype(jnp.float32)).astype(jnp.bfloat16)
        applied = exchange(chip_sum.reshape(chips, share, width)).astype(jnp.float32).sum(axis=0) * scaled_mask
        updated = applied if iteration == 0 else 2.0 * applied - outputs[-2]
        outputs.append(updated)
        if iteration + 1 < STEPS:
            rows = updated.astype(jnp.bfloat16)
            even_rows = send(rows, even)
            three = jnp.stack([rows, even_rows, send(rows, odd)])
            near = spread(three)
            far = send(near, partner_core)
            wholes = []
    return (outputs[-2][None], outputs[-1][None])


def solution(mesh):
    in_specs = (
        P("sec", None, None),
        P("sec", "ops", None, None),
        P("sec", "ops", None, None),
        P("sec", "ops"),
        P(),
    )
    out_specs = (P("sec", "ops", None), P("sec", "ops", None))
    return jax.shard_map(
        on_device, mesh=mesh, in_specs=in_specs, out_specs=out_specs, check_vma=False
    )
```

time: 110 us -> 109 us (level)
  waiting for transfers between devices: 27.9 us -> 23.6 us
  Pallas kernels: 17.5 us -> 19.1 us
    ppermute x9, waiting for transfers between devices: 27.9 us -> 23.6 us  [send(): return lax.ppermute(block, AXES, where)]
    pallas_call x4 -> x7, Pallas kernels: 17.5 us -> 19.1 us  [the longest x2 8.46 us: other_rows(): pl.pallas_call(functools.partial(other_kernel, len(wholes)), in_specs=[SM...]
  transfers between devices with their start and end apart: 10 -> 10, of which waited for: 8 -> 4; matrix products, arithmetic and copies ran while one was open for 0% -> 0% of each run, Pallas kernels for 1% -> 9%
where the time goes in v1:
time: 109 us; the launch traced here: 107 us
  blocking collectives  46.2 us (42%)
  waiting for transfers between devices  23.6 us (22%)
  Pallas kernels  19.1 us (18%)
  starting transfers between devices  15.2 us (14%)
  other arithmetic  1.65 us (2%)
    all_to_all x3, blocking collectives, exchange(): lax.all_to_all(tiles, 'ops', 0, 0, axis_index_groups=same_core, tiled=True)  46.2 us
    ppermute x9, waiting for transfers between devices, send(): return lax.ppermute(block, AXES, where)  23.6 us
    ppermute x9, starting transfers between devices, send(): return lax.ppermute(block, AXES, where)  10 us
    pallas_call x2, Pallas kernels, other_rows(): pl.pallas_call(functools.partial(other_kernel, len(wholes)), in_specs=[SM...  8.46 us
    pallas_call x2, Pallas kernels, mine_rows(): pl.pallas_call(mine_kernel, in_specs=[SMEM, VMEM, VMEM, VMEM], out_specs=...  5.93 us
    all_to_all x1, starting transfers between devices, exchange(): lax.all_to_all(tiles, 'ops', 0, 0, axis_index_groups=same_core, tiled=True)  5.2 us
    pallas_call x1, Pallas kernels, prepare_rest(): pl.pallas_call(functools.partial(rest_kernel, norm_scale), in_specs=[HBM,...  2.36 us
    pallas_call x2, Pallas kernels, masked_rows(): pl.pallas_call(functools.partial(cut_kernel, first_row), in_specs=[HBM, H...  2.32 us
  transfers between devices with their start and end apart: 10, of which 4 were waited for; matrix products, arithmetic and copies ran while one was open for 0% of the time, Pallas kernels for 9%

profile of v1, /device:TPU:128, one launch (start us, length us, event | category | flops | bytes accessed | tf_op | source)
XLA Modules:
  0.0 107.5 jit_solution(9345496030152729971)
XLA Ops:
  0.6 1.1 shard_map.69
  1.7 4.0 %collective-permute-start = (bf16[40,640]{1,0:T(8,128)(2,1)S(1)}, bf16[40,640]{1,0:T(8,128)(2,1)S(1)}, u32[]{:S(2)}, u32[]{:S(2)}) collective-permute-start(bf16[40,640]{1,0:T(8,128)(2,1)S(1)} %shard_map.69), channel_id=1, source_target_pairs={{1,2},{2,1},{3,4},{4,3},{5,6},{6,5},{7,8},{8,7},{9,10},{10,9},{11,... | collective-permute-start | bytes 153608 | tf_op jit(solution)/shard_map/ppermute | solution.py:249
  5.7 6.3 %collective-permute-done = bf16[40,640]{1,0:T(8,128)(2,1)S(1)} collective-permute-done((bf16[40,640]{1,0:T(8,128)(2,1)S(1)}, bf16[40,640]{1,0:T(8,128)(2,1)S(1)}, u32[]{:S(2)}, u32[]{:S(2)}) %collective-permute-start) | collective-permute-done | bytes 51232 | tf_op jit(solution)/shard_map/ppermute | solution.py:249
  12.0 0.8 broadcast_in_dim.8
  12.8 5.2 %all-to-all-start = ((bf16[8,40,640]{2,1,0:T(8,128)(2,1)}), bf16[8,40,640]{2,1,0:T(8,128)(2,1)S(1)}, u32[]{:S(2)}, u32[]{:S(2)}) async-start(bf16[8,40,640]{2,1,0:T(8,128)(2,1)} %broadcast_in_dim.8), calls=%async_computation | async-start | bytes 819200 | tf_op jit(solution)/shard_map/all_to_all | solution.py:252
  18.0 1.3 %shard_map.70 = bf16[320,640]{1,0:T(8,128)(2,1)S(1)} custom-call(s32[16]{0:T(128)} %sizes_ref.5, f32[640,640]{1,0:T(8,128)} %bitcast.13), custom_call_target="tpu_custom_call" | custom-call | flops 204800 | bytes 1228800 | tf_op jit(solution)/shard_map/pallas_call | solution.py:58
  19.4 9.2 %collective-permute-done.1.refs_1_ = bf16[320,640]{1,0:T(8,128)(2,1)S(1)} collective-permute-done((bf16[320,640]{1,0:T(8,128)(2,1)S(1)}, bf16[320,640]{1,0:T(8,128)(2,1)S(1)}, u32[]{:S(2)}, u32[]{:S(2)}) %collective-permute-start.1) | collective-permute-done | bytes 409632 | tf_op jit(solution)/shard_map/ppermute | solution.py:249
  28.6 0.5 collective-permute-start.3
  29.2 2.4 %shard_map.68 = (bf16[640,640]{1,0:T(8,128)(2,1)}, f32[40,640]{1,0:T(8,128)S(1)}, f32[40,640]{1,0:T(8,128)S(1)}, bf16[3,640,640]{2,1,0:T(8,128)(2,1)S(1)}) custom-call(s32[16]{0:T(128)} %sizes_ref.5, f32[640,640]{1,0:T(8,128)S(1)} %bitcast.14, bf16[3,640,640]{2,1,0:T(8,128)(2,1)} %bitcast.17), custom_call_target="tpu_custom_call" | custom-call | flops 409600 | bytes 7372800 | tf_op jit(solution)/shard_map/pallas_call | solution.py:105
  31.6 4.8 %shard_map.71 = (bf16[320,640]{1,0:T(8,128)(2,1)S(1)}, bf16[3,640,640]{2,1,0:T(8,128)(2,1)S(1)}, bf16[3,640,640]{2,1,0:T(8,128)(2,1)S(1)}) custom-call(s32[1,3]{1,0:T(1,128)S(1)} %copy-done.1, bf16[640,640]{1,0:T(8,128)(2,1)} %get-tuple-element.14.refs_0_, bf16[320,640]{1,0:T(8,128)(2,1)S(1)} %collective-permute-done.1.refs_1_, ...), custom_call_target="tpu_custom_call" | custom-call | flops 1572864000 | bytes 4915200 | tf_op jit(solution)/shard_map/pallas_call | solution.py:205
  36.5 3.0 %shard_map.72 = f32[320,640]{1,0:T(8,128)S(1)} custom-call(s32[1,3]{1,0:T(1,128)S(1)} %copy-done.1, bf16[3,640,640]{2,1,0:T(8,128)(2,1)S(1)} %get-tuple-element.18.field_ref, bf16[3,640,640]{2,1,0:T(8,128)(2,1)S(1)} %get-tuple-element.17.refs_5_.left_ref.refs_2_, bf16[3,640,640]{2,1,0:T(8,128)(2,1)S(1)} %get-tuple-element.19.right_ref), custom_call_target="tpu_custom_call" | custom-call | flops 1572864000 | bytes 4915200 | tf_op jit(solution)/shard_map/pallas_call | solution.py:226
  39.4 0.1 add_convert_fusion.1
  39.5 14.8 %all_to_all.20 = bf16[8,40,640]{2,1,0:T(8,128)(2,1)S(1)} all-to-all(bf16[8,40,640]{2,1,0:T(8,128)(2,1)S(1)} %bitcast.18), channel_id=1, replica_groups={{0,32,64,96,128,160,192,224},{16,48,80,112,144,176,208,240},{1,33,65,97..., dimensions={0} | all-to-all | bytes 819200 | tf_op jit(solution)/shard_map/all_to_all | solution.py:252
  54.4 0.7 multiply_convert_fusion
  55.1 5.0 %collective-permute-start.6 = (bf16[40,640]{1,0:T(8,128)(2,1)S(1)}, bf16[40,640]{1,0:T(8,128)(2,1)S(1)}, u32[]{:S(2)}, u32[]{:S(2)}) collective-permute-start(bf16[40,640]{1,0:T(8,128)(2,1)S(1)} %get-tuple-element.26), channel_id=1, source_target_pairs={{1,2},{2,1},{3,4},{4,3},{5,6},{6,5},{7,8},{8,7},{9,10},{10,9},{11,... | collective-permute-start | bytes 153608 | tf_op jit(solution)/shard_map/ppermute | solution.py:249
  60.2 5.1 %collective-permute-done.6 = bf16[40,640]{1,0:T(8,128)(2,1)S(1)} collective-permute-done((bf16[40,640]{1,0:T(8,128)(2,1)S(1)}, bf16[40,640]{1,0:T(8,128)(2,1)S(1)}, u32[]{:S(2)}, u32[]{:S(2)}) %collective-permute-start.6) | collective-permute-done | bytes 51232 | tf_op jit(solution)/shard_map/ppermute | solution.py:249
  65.3 0.1 broadcast_in_dim.20
  65.4 19.2 %all_to_all.21.refs_0_ = bf16[8,3,40,640]{3,2,1,0:T(8,128)(2,1)S(1)} all-to-all(bf16[8,3,40,640]{3,2,1,0:T(8,128)(2,1)S(1)} %broadcast_in_dim.20), channel_id=1, replica_groups={{0,32,64,96,128,160,192,224},{16,48,80,112,144,176,208,240},{1,33,65,97..., dimensions={0} | all-to-all | bytes 2457600 | tf_op jit(solution)/shard_map/all_to_all | solution.py:252
  84.7 2.9 %collective-permute-done.7.refs_1_ = bf16[8,3,40,640]{3,2,1,0:T(8,128)(2,1)S(1)} collective-permute-done((bf16[8,3,40,640]{3,2,1,0:T(8,128)(2,1)S(1)}, bf16[8,3,40,640]{3,2,1,0:T(8,128)(2,1)S(1)}, u32[]{:S(2)}, u32[]{:S(2)}) %collective-permute-start.7) | collective-permute-done | bytes 1228832 | tf_op jit(solution)/shard_map/ppermute | solution.py:249
  87.6 3.7 %shard_map.73 = (bf16[320,640]{1,0:T(8,128)(2,1)S(1)}, bf16[3,640,640]{2,1,0:T(8,128)(2,1)S(1)}, bf16[3,640,640]{2,1,0:T(8,128)(2,1)S(1)}) custom-call(s32[1,3]{1,0:T(1,128)S(1)} %copy-done.1, bf16[8,3,40,640]{3,2,1,0:T(8,128)(2,1)S(1)} %all_to_all.21.refs_0_, bf16[8,3,40,640]{3,2,1,0:T(8,128)(2,1)S(1)} %collective-permute-done.7.refs_1_, ...), custom_call_target="tpu_custom_call" | custom-call | flops 1572864000 | bytes 4915200 | tf_op jit(solution)/shard_map/pallas_call | solution.py:205
  91.3 0.2 collective-permute-start.8
  91.5 3.0 %shard_map.74 = f32[320,640]{1,0:T(8,128)S(1)} custom-call(s32[1,3]{1,0:T(1,128)S(1)} %copy-done.1, bf16[3,640,640]{2,1,0:T(8,128)(2,1)S(1)} %get-tuple-element.22.field_ref, bf16[3,640,640]{2,1,0:T(8,128)(2,1)S(1)} %get-tuple-element.17.refs_5_.left_ref.refs_2_, bf16[3,640,640]{2,1,0:T(8,128)(2,1)S(1)} %get-tuple-element.23.right_ref), custom_call_target="tpu_custom_call" | custom-call | flops 1572864000 | bytes 4915200 | tf_op jit(solution)/shard_map/pallas_call | solution.py:226
  94.6 12.2 %all_to_all.22 = bf16[8,40,640]{2,1,0:T(8,128)(2,1)S(1)} all-to-all(bf16[8,40,640]{2,1,0:T(8,128)(2,1)S(1)} %bitcast.19), channel_id=1, replica_groups={{0,32,64,96,128,160,192,224},{16,48,80,112,144,176,208,240},{1,33,65,97..., dimensions={0} | all-to-all | bytes 819200 | tf_op jit(solution)/shard_map/all_to_all | solution.py:252
  106.8 0.7 subtract_bitcast_fusion
  (19 shorter events, 0.5 us)
Async XLA Ops:
  0.6 28.5 %copy-start = (f32[1,640,640]{2,1,0:T(8,128)S(1)}, f32[1,640,640]{2,1,0:T(8,128)}, u32[]{:S(2)}) copy-start(f32[1,640,640]{2,1,0:T(8,128)} %param.5) | copy-start | bytes 4915204
  1.7 10.3 %collective-permute-start = (bf16[40,640]{1,0:T(8,128)(2,1)S(1)}, bf16[40,640]{1,0:T(8,128)(2,1)S(1)}, u32[]{:S(2)}, u32[]{:S(2)}) collective-permute-start(bf16[40,640]{1,0:T(8,128)(2,1)S(1)} %shard_map.69), channel_id=1, source_target_pairs={{1,2},{2,1},{3,4},{4,3},{5,6},{6,5},{7,8},{8,7},{9,10},{10,9},{11,... | collective-permute-start | bytes 153608 | tf_op jit(solution)/shard_map/ppermute | solution.py:249
  12.8 15.8 %all-to-all-start = ((bf16[8,40,640]{2,1,0:T(8,128)(2,1)}), bf16[8,40,640]{2,1,0:T(8,128)(2,1)S(1)}, u32[]{:S(2)}, u32[]{:S(2)}) async-start(bf16[8,40,640]{2,1,0:T(8,128)(2,1)} %broadcast_in_dim.8), calls=%async_computation | async-start | bytes 819200 | tf_op jit(solution)/shard_map/all_to_all | solution.py:252
  19.3 12.3 %copy-start.1 = (s32[1,3]{1,0:T(1,128)S(1)}, s32[1,3]{1,0:T(1,128)}, u32[]{:S(2)}) copy-start(s32[1,3]{1,0:T(1,128)} %charge_ref.7) | copy-start | bytes 40
  19.3 9.3 %collective-permute-start.1 = (bf16[320,640]{1,0:T(8,128)(2,1)S(1)}, bf16[320,640]{1,0:T(8,128)(2,1)S(1)}, u32[]{:S(2)}, u32[]{:S(2)}) collective-permute-start(bf16[320,640]{1,0:T(8,128)(2,1)S(1)} %shard_map.70), channel_id=1, source_target_pairs={{0,1},{1,0},{2,3},{3,2},{4,5},{5,4},{6,7},{7,6},{8,9},{9,8},{10,11... | collective-permute-start | bytes 1228808 | tf_op jit(solution)/shard_map/ppermute | solution.py:249
  28.6 2.9 %collective-permute-start.2 = (bf16[320,640]{1,0:T(8,128)(2,1)S(1)}, bf16[320,640]{1,0:T(8,128)(2,1)S(1)}, u32[]{:S(2)}, u32[]{:S(2)}) collective-permute-start(bf16[320,640]{1,0:T(8,128)(2,1)S(1)} %collective-permute-done.1.refs_1_), channel_id=1, source_target_pairs={{0,16},{1,17},{2,18},{3,19},{4,20},{5,21},{6,22},{7,23},{8,24},{9,... | collective-permute-start | bytes 1228808 | tf_op jit(solution)/shard_map/ppermute | solution.py:249
  28.6 2.9 %collective-permute-start.3 = (bf16[8,40,640]{2,1,0:T(8,128)(2,1)S(1)}, bf16[8,40,640]{2,1,0:T(8,128)(2,1)S(1)}, u32[]{:S(2)}, u32[]{:S(2)}) collective-permute-start(bf16[8,40,640]{2,1,0:T(8,128)(2,1)S(1)} %all-to-all-done.refs_3_), channel_id=1, source_target_pairs={{0,16},{1,17},{2,18},{3,19},{4,20},{5,21},{6,22},{7,23},{8,24},{9,... | collective-permute-start | bytes 1228808 | tf_op jit(solution)/shard_map/ppermute | solution.py:249
  36.4 3.1 %collective-permute-start.4 = (bf16[320,640]{1,0:T(8,128)(2,1)S(1)}, bf16[320,640]{1,0:T(8,128)(2,1)S(1)}, u32[]{:S(2)}, u32[]{:S(2)}) collective-permute-start(bf16[320,640]{1,0:T(8,128)(2,1)S(1)} %get-tuple-element.20), channel_id=1, source_target_pairs={{0,16},{1,17},{2,18},{3,19},{4,20},{5,21},{6,22},{7,23},{8,24},{9,... | collective-permute-start | bytes 1228808 | tf_op jit(solution)/shard_map/ppermute | solution.py:249
  55.1 10.2 %collective-permute-start.6 = (bf16[40,640]{1,0:T(8,128)(2,1)S(1)}, bf16[40,640]{1,0:T(8,128)(2,1)S(1)}, u32[]{:S(2)}, u32[]{:S(2)}) collective-permute-start(bf16[40,640]{1,0:T(8,128)(2,1)S(1)} %get-tuple-element.26), channel_id=1, source_target_pairs={{1,2},{2,1},{3,4},{4,3},{5,6},{6,5},{7,8},{8,7},{9,10},{10,9},{11,... | collective-permute-start | bytes 153608 | tf_op jit(solution)/shard_map/ppermute | solution.py:249
  60.1 5.2 %collective-permute-start.5 = (bf16[40,640]{1,0:T(8,128)(2,1)S(1)}, bf16[40,640]{1,0:T(8,128)(2,1)S(1)}, u32[]{:S(2)}, u32[]{:S(2)}) collective-permute-start(bf16[40,640]{1,0:T(8,128)(2,1)S(1)} %get-tuple-element.26), channel_id=1, source_target_pairs={{0,1},{1,0},{2,3},{3,2},{4,5},{5,4},{6,7},{7,6},{8,9},{9,8},{10,11... | collective-permute-start | bytes 153608 | tf_op jit(solution)/shard_map/ppermute | solution.py:249
  84.7 2.9 %collective-permute-start.7 = (bf16[8,3,40,640]{3,2,1,0:T(8,128)(2,1)S(1)}, bf16[8,3,40,640]{3,2,1,0:T(8,128)(2,1)S(1)}, u32[]{:S(2)}, u32[]{:S(2)}) collective-permute-start(bf16[8,3,40,640]{3,2,1,0:T(8,128)(2,1)S(1)} %all_to_all.21.refs_0_), channel_id=1, source_target_pairs={{0,16},{1,17},{2,18},{3,19},{4,20},{5,21},{6,22},{7,23},{8,24},{9,... | collective-permute-start | bytes 3686408 | tf_op jit(solution)/shard_map/ppermute | solution.py:249
  91.3 3.2 %collective-permute-start.8 = (bf16[320,640]{1,0:T(8,128)(2,1)S(1)}, bf16[320,640]{1,0:T(8,128)(2,1)S(1)}, u32[]{:S(2)}, u32[]{:S(2)}) collective-permute-start(bf16[320,640]{1,0:T(8,128)(2,1)S(1)} %get-tuple-element.24), channel_id=1, source_target_pairs={{0,16},{1,17},{2,18},{3,19},{4,20},{5,21},{6,22},{7,23},{8,24},{9,... | collective-permute-start | bytes 1228808 | tf_op jit(solution)/shard_map/ppermute | solution.py:249

commit v2 on v1

--- a/solution.py
+++ b/solution.py
@@ -13,7 +13,6 @@
 AXES = ("ops", "sec")
 VMEM = pl.BlockSpec(memory_space=pltpu.VMEM)
 SMEM = pl.BlockSpec(memory_space=pltpu.SMEM)
-ANY = pl.BlockSpec(memory_space=pl.ANY)
 HBM = pl.BlockSpec(memory_space=pltpu.HBM)
 MIB = 2**20
 
@@ -70,7 +69,7 @@
     )(in_hbm(sizes), in_hbm(wave))
 
 
-def rest_kernel(norm_scale, sizes_ref, wave_ref, left_hbm, own_hbm, start_ref, mask_ref, left_ref, own_buf, sizes_buf, sems, own_sem, sizes_sem):
+def rest_kernel(norm_scale, sizes_ref, wave_ref, left_hbm, own_ref, start_ref, mask_ref, left_ref, sizes_buf, sems, sizes_sem):
     share, width = start_ref.shape
     count, owners, blocks = left_ref.shape[0], 2, width // share // 2
     copies = []
@@ -90,13 +89,11 @@
     sizes_copy.wait()
     size = sizes_buf[lax.axis_index("sec")]
     first = pl.multiple_of(share * lax.axis_index("ops"), 8)
-    own_buf[...] = (wave_ref[...] * live(size, 0, width, width)).astype(jnp.bfloat16)
-    own_copy = pltpu.make_async_copy(own_buf, own_hbm, own_sem)
-    own_copy.start()
+    own_ref[...] = (wave_ref[...] * live(size, 0, width, width)).astype(jnp.bfloat16)
     mask = live(size, first, share, width)
     start_ref[...] = wave_ref[pl.ds(first, share), :] * mask
     mask_ref[...] = mask * norm_scale
-    for copy in copies + [own_copy]:
+    for copy in copies:
         copy.wait()
 
 
@@ -105,18 +102,16 @@
     return pl.pallas_call(
         functools.partial(rest_kernel, norm_scale),
         in_specs=[HBM, VMEM, HBM],
-        out_specs=[HBM] + [VMEM] * 3,
+        out_specs=[VMEM] * 4,
         out_shape=[
-            pltpu.HBM((width, width), jnp.bfloat16),
+            jax.ShapeDtypeStruct((width, width), jnp.bfloat16),
             jax.ShapeDtypeStruct((share, width), jnp.float32),
             jax.ShapeDtypeStruct((share, width), jnp.float32),
             jax.ShapeDtypeStruct(left.shape, left.dtype),
         ],
         scratch_shapes=[
-            pltpu.VMEM((width, width), jnp.bfloat16),
             pltpu.SMEM(sizes.shape, jnp.int32),
             pltpu.SemaphoreType.DMA((left.shape[0] * width // share,)),
-            pltpu.SemaphoreType.DMA,
             pltpu.SemaphoreType.DMA,
         ],
         compiler_params=pltpu.CompilerParams(vmem_limit_bytes=12 * MIB),
@@ -149,29 +144,23 @@
 
 def other_kernel(n_whole, charge_ref, *refs):
     wholes, (near_ref, far_ref, left_ref, right_hbm, other_ref, field_ref, right_ref) = refs[:n_whole], refs[n_whole : n_whole + 7]
-    half_ref, right_sem, whole_sems = refs[n_whole + 7 :]
+    half_ref, right_sem = refs[n_whole + 7 :]
     width = field_ref.shape[1]
     half = width // 2
     core = lax.rem(lax.axis_index("ops"), 2)
 
-    copies = []
-    for k, ref in enumerate(wholes):
-        if k == 0:
-            target = field_ref.at[0]
-        else:
-            owner = core if k == 1 else 1 - core
-            target = field_ref.at[1, pl.ds(pl.multiple_of(half * owner, 16), half), :]
-        copies.append(pltpu.make_async_copy(ref, target, whole_sems.at[k]))
     right_copy = pltpu.make_async_copy(right_hbm, right_ref, right_sem)
-    for copy in copies or [right_copy]:
-        copy.start()
-
+    right_copy.start()
     blocks = near_ref.shape[0]
     share = half // blocks
     for c in range(2):
 
         @pl.when(core == c)
         def _():
+            if n_whole:
+                field_ref[0] = wholes[0][...]
+                field_ref[1, half * c : half * (c + 1), :] = wholes[1][...]
+                field_ref[1, half * (1 - c) : half * (2 - c), :] = wholes[2][...]
             for part, owner in ((near_ref, c), (far_ref, 1 - c)):
                 for block in range(blocks):
                     if n_whole:
@@ -182,10 +171,6 @@
                         for slot in range(3):
                             field_ref[slot, row : row + share, :] = part[block, slot]
 
-    for copy in copies:
-        copy.wait()
-    if copies:
-        right_copy.start()
     other_ref[...] = products(
         charge_ref, field_ref, left_ref, right_ref, half_ref, 1 - core, right_copy.wait
     ).astype(jnp.bfloat16)
@@ -204,7 +189,7 @@
     count, width, _ = left.shape
     return pl.pallas_call(
         functools.partial(other_kernel, len(wholes)),
-        in_specs=[SMEM] + [ANY] * len(wholes) + [VMEM, VMEM, VMEM, HBM],
+        in_specs=[SMEM] + [VMEM] * len(wholes) + [VMEM, VMEM, VMEM, HBM],
         out_specs=[VMEM] * 3,
         out_shape=[
             jax.ShapeDtypeStruct((width // 2, width), jnp.bfloat16),
@@ -214,7 +199,6 @@
         scratch_shapes=[
             pltpu.VMEM((width // 2, count * width), jnp.bfloat16),
             pltpu.SemaphoreType.DMA,
-            pltpu.SemaphoreType.DMA((3,)),
         ],
         compiler_params=pltpu.CompilerParams(vmem_limit_bytes=20 * MIB),
         cost_estimate=cost(count, width),
@@ -264,10 +248,10 @@
         sector_sizes, wave, left_ops[0], share, norm_scale
     )
     near = spread(odd_rows)
-    near, even_near = lax.optimization_barrier((near, even_near))
+    gate = near[0, :8, :128].astype(jnp.float32)
     even_far = send(even_near, partner_core)
     far = send(near, partner_core)
-    wholes = [in_hbm(own), even_near, even_far]
+    wholes = [own, even_near, even_far, gate]
 
     outputs = [start_rows]
     for iteration in range(STEPS):

time: 109 us -> 107 us (0.982)
  Pallas kernels: 19.1 us -> 17.6 us
    pallas_call x2, Pallas kernels: 8.46 us -> 7.24 us  [other_rows(): pl.pallas_call(functools.partial(other_kernel, len(wholes)), in_specs=[SM...]
where the time goes in v2:
time: 107 us; the launch traced here: 106 us
  blocking collectives  46.2 us (43%)
  waiting for transfers between devices  23.6 us (22%)
  Pallas kernels  17.6 us (16%)
  starting transfers between devices  15.2 us (14%)
  other arithmetic  1.64 us (2%)
    all_to_all x3, blocking collectives, exchange(): lax.all_to_all(tiles, 'ops', 0, 0, axis_index_groups=same_core, tiled=True)  46.2 us
    ppermute x9, waiting for transfers between devices, send(): return lax.ppermute(block, AXES, where)  23.6 us
    ppermute x9, starting transfers between devices, send(): return lax.ppermute(block, AXES, where)  10 us
    pallas_call x2, Pallas kernels, other_rows(): pl.pallas_call(functools.partial(other_kernel, len(wholes)), in_specs=[SM...  7.24 us
    pallas_call x2, Pallas kernels, mine_rows(): pl.pallas_call(mine_kernel, in_specs=[SMEM, VMEM, VMEM, VMEM], out_specs=...  5.95 us
    all_to_all x1, starting transfers between devices, exchange(): lax.all_to_all(tiles, 'ops', 0, 0, axis_index_groups=same_core, tiled=True)  5.2 us
    pallas_call x2, Pallas kernels, masked_rows(): pl.pallas_call(functools.partial(cut_kernel, first_row), in_specs=[HBM, H...  2.32 us
  transfers between devices with their start and end apart: 10, of which 4 were waited for; matrix products, arithmetic and copies ran while one was open for 0% of the time, Pallas kernels for 9%

profile of v2, /device:TPU:128, one launch (start us, length us, event | category | flops | bytes accessed | tf_op | source)
XLA Modules:
  0.0 106.0 jit_solution(8702058063915290370)
XLA Ops:
  0.6 1.1 %shard_map.70 = bf16[40,640]{1,0:T(8,128)(2,1)S(1)} custom-call(s32[16]{0:T(128)} %sizes_ref.5, f32[640,640]{1,0:T(8,128)} %bitcast.17), custom_call_target="tpu_custom_call" | custom-call | flops 25600 | bytes 153600 | tf_op jit(solution)/shard_map/pallas_call | solution.py:57
  1.7 4.0 %collective-permute-start.2 = (bf16[40,640]{1,0:T(8,128)(2,1)S(1)}, bf16[40,640]{1,0:T(8,128)(2,1)S(1)}, u32[]{:S(2)}, u32[]{:S(2)}) collective-permute-start(bf16[40,640]{1,0:T(8,128)(2,1)S(1)} %shard_map.70), channel_id=1, source_target_pairs={{1,2},{2,1},{3,4},{4,3},{5,6},{6,5},{7,8},{8,7},{9,10},{10,9},{11,... | collective-permute-start | bytes 153608 | tf_op jit(solution)/shard_map/ppermute | solution.py:233
  5.7 6.3 %collective-permute-done.2 = bf16[40,640]{1,0:T(8,128)(2,1)S(1)} collective-permute-done((bf16[40,640]{1,0:T(8,128)(2,1)S(1)}, bf16[40,640]{1,0:T(8,128)(2,1)S(1)}, u32[]{:S(2)}, u32[]{:S(2)}) %collective-permute-start.2) | collective-permute-done | bytes 51232 | tf_op jit(solution)/shard_map/ppermute | solution.py:233
  12.0 0.8 broadcast_in_dim.8
  12.8 5.2 %all-to-all-start = ((bf16[8,40,640]{2,1,0:T(8,128)(2,1)}), bf16[8,40,640]{2,1,0:T(8,128)(2,1)S(1)}, u32[]{:S(2)}, u32[]{:S(2)}) async-start(bf16[8,40,640]{2,1,0:T(8,128)(2,1)} %broadcast_in_dim.8), calls=%async_computation | async-start | bytes 819200 | tf_op jit(solution)/shard_map/all_to_all | solution.py:236
  18.0 1.3 %shard_map.69 = bf16[320,640]{1,0:T(8,128)(2,1)S(1)} custom-call(s32[16]{0:T(128)} %sizes_ref.5, f32[640,640]{1,0:T(8,128)} %bitcast.18), custom_call_target="tpu_custom_call" | custom-call | flops 204800 | bytes 1228800 | tf_op jit(solution)/shard_map/pallas_call | solution.py:57
  19.4 9.2 %collective-permute-done.refs_1_ = bf16[320,640]{1,0:T(8,128)(2,1)S(1)} collective-permute-done((bf16[320,640]{1,0:T(8,128)(2,1)S(1)}, bf16[320,640]{1,0:T(8,128)(2,1)S(1)}, u32[]{:S(2)}, u32[]{:S(2)}) %collective-permute-start) | collective-permute-done | bytes 409632 | tf_op jit(solution)/shard_map/ppermute | solution.py:233
  28.6 0.5 collective-permute-start.3
  29.2 2.1 %shard_map.68 = (bf16[640,640]{1,0:T(8,128)(2,1)S(1)}, f32[40,640]{1,0:T(8,128)S(1)}, f32[40,640]{1,0:T(8,128)S(1)}, bf16[3,640,640]{2,1,0:T(8,128)(2,1)S(1)}) custom-call(s32[16]{0:T(128)} %sizes_ref.5, f32[640,640]{1,0:T(8,128)S(1)} %bitcast.19, bf16[3,640,640]{2,1,0:T(8,128)(2,1)} %bitcast.22), custom_call_target="tpu_custom_call" | custom-call | flops 409600 | bytes 7372800 | tf_op jit(solution)/shard_map/pallas_call | solution.py:102
  31.3 3.6 %shard_map.71 = (bf16[320,640]{1,0:T(8,128)(2,1)S(1)}, bf16[3,640,640]{2,1,0:T(8,128)(2,1)S(1)}, bf16[3,640,640]{2,1,0:T(8,128)(2,1)S(1)}) custom-call(s32[1,3]{1,0:T(1,128)S(1)} %copy-done.1, bf16[640,640]{1,0:T(8,128)(2,1)S(1)} %get-tuple-element.12.refs_0_, bf16[320,640]{1,0:T(8,128)(2,1)S(1)} %collective-permute-done.refs_1_, ...), custom_call_target="tpu_custom_call" | custom-call | flops 1572864000 | bytes 4915200 | tf_op jit(solution)/shard_map/pallas_call | solution.py:190
  34.9 0.1 collective-permute-start.4
  35.0 3.0 %shard_map.72 = f32[320,640]{1,0:T(8,128)S(1)} custom-call(s32[1,3]{1,0:T(1,128)S(1)} %copy-done.1, bf16[3,640,640]{2,1,0:T(8,128)(2,1)S(1)} %get-tuple-element.14.field_ref, bf16[3,640,640]{2,1,0:T(8,128)(2,1)S(1)} %get-tuple-element.13.refs_6_.left_ref.refs_2_, bf16[3,640,640]{2,1,0:T(8,128)(2,1)S(1)} %get-tuple-element.15.right_ref), custom_call_target="tpu_custom_call" | custom-call | flops 1572864000 | bytes 4915200 | tf_op jit(solution)/shard_map/pallas_call | solution.py:210
  38.1 14.8 %all_to_all.20 = bf16[8,40,640]{2,1,0:T(8,128)(2,1)S(1)} all-to-all(bf16[8,40,640]{2,1,0:T(8,128)(2,1)S(1)} %bitcast.23), channel_id=1, replica_groups={{0,32,64,96,128,160,192,224},{16,48,80,112,144,176,208,240},{1,33,65,97..., dimensions={0} | all-to-all | bytes 819200 | tf_op jit(solution)/shard_map/all_to_all | solution.py:236
  52.9 0.7 multiply_convert_fusion
  53.6 5.0 %collective-permute-start.6 = (bf16[40,640]{1,0:T(8,128)(2,1)S(1)}, bf16[40,640]{1,0:T(8,128)(2,1)S(1)}, u32[]{:S(2)}, u32[]{:S(2)}) collective-permute-start(bf16[40,640]{1,0:T(8,128)(2,1)S(1)} %get-tuple-element.22), channel_id=1, source_target_pairs={{1,2},{2,1},{3,4},{4,3},{5,6},{6,5},{7,8},{8,7},{9,10},{10,9},{11,... | collective-permute-start | bytes 153608 | tf_op jit(solution)/shard_map/ppermute | solution.py:233
  58.7 5.1 %collective-permute-done.6 = bf16[40,640]{1,0:T(8,128)(2,1)S(1)} collective-permute-done((bf16[40,640]{1,0:T(8,128)(2,1)S(1)}, bf16[40,640]{1,0:T(8,128)(2,1)S(1)}, u32[]{:S(2)}, u32[]{:S(2)}) %collective-permute-start.6) | collective-permute-done | bytes 51232 | tf_op jit(solution)/shard_map/ppermute | solution.py:233
  64.0 19.2 %all_to_all.21.refs_0_ = bf16[8,3,40,640]{3,2,1,0:T(8,128)(2,1)S(1)} all-to-all(bf16[8,3,40,640]{3,2,1,0:T(8,128)(2,1)S(1)} %broadcast_in_dim.20), channel_id=1, replica_groups={{0,32,64,96,128,160,192,224},{16,48,80,112,144,176,208,240},{1,33,65,97..., dimensions={0} | all-to-all | bytes 2457600 | tf_op jit(solution)/shard_map/all_to_all | solution.py:236
  83.2 2.9 %collective-permute-done.7.refs_1_ = bf16[8,3,40,640]{3,2,1,0:T(8,128)(2,1)S(1)} collective-permute-done((bf16[8,3,40,640]{3,2,1,0:T(8,128)(2,1)S(1)}, bf16[8,3,40,640]{3,2,1,0:T(8,128)(2,1)S(1)}, u32[]{:S(2)}, u32[]{:S(2)}) %collective-permute-start.7) | collective-permute-done | bytes 1228832 | tf_op jit(solution)/shard_map/ppermute | solution.py:233
  86.1 3.6 %shard_map.73 = (bf16[320,640]{1,0:T(8,128)(2,1)S(1)}, bf16[3,640,640]{2,1,0:T(8,128)(2,1)S(1)}, bf16[3,640,640]{2,1,0:T(8,128)(2,1)S(1)}) custom-call(s32[1,3]{1,0:T(1,128)S(1)} %copy-done.1, bf16[8,3,40,640]{3,2,1,0:T(8,128)(2,1)S(1)} %all_to_all.21.refs_0_, bf16[8,3,40,640]{3,2,1,0:T(8,128)(2,1)S(1)} %collective-permute-done.7.refs_1_, ...), custom_call_target="tpu_custom_call" | custom-call | flops 1572864000 | bytes 4915200 | tf_op jit(solution)/shard_map/pallas_call | solution.py:190
  89.8 0.2 collective-permute-start.8
  90.0 3.0 %shard_map.74 = f32[320,640]{1,0:T(8,128)S(1)} custom-call(s32[1,3]{1,0:T(1,128)S(1)} %copy-done.1, bf16[3,640,640]{2,1,0:T(8,128)(2,1)S(1)} %get-tuple-element.18.field_ref, bf16[3,640,640]{2,1,0:T(8,128)(2,1)S(1)} %get-tuple-element.13.refs_6_.left_ref.refs_2_, bf16[3,640,640]{2,1,0:T(8,128)(2,1)S(1)} %get-tuple-element.19.right_ref), custom_call_target="tpu_custom_call" | custom-call | flops 1572864000 | bytes 4915200 | tf_op jit(solution)/shard_map/pallas_call | solution.py:210
  93.0 0.1 add_convert_fusion
  93.1 12.2 %all_to_all.22 = bf16[8,40,640]{2,1,0:T(8,128)(2,1)S(1)} all-to-all(bf16[8,40,640]{2,1,0:T(8,128)(2,1)S(1)} %bitcast.24), channel_id=1, replica_groups={{0,32,64,96,128,160,192,224},{16,48,80,112,144,176,208,240},{1,33,65,97..., dimensions={0} | all-to-all | bytes 819200 | tf_op jit(solution)/shard_map/all_to_all | solution.py:236
  105.3 0.7 subtract_bitcast_fusion
  (20 shorter events, 0.5 us)
Async XLA Ops:
  0.6 28.5 %copy-start = (f32[1,640,640]{2,1,0:T(8,128)S(1)}, f32[1,640,640]{2,1,0:T(8,128)}, u32[]{:S(2)}) copy-start(f32[1,640,640]{2,1,0:T(8,128)} %param.5) | copy-start | bytes 4915204
  1.7 10.3 %collective-permute-start.2 = (bf16[40,640]{1,0:T(8,128)(2,1)S(1)}, bf16[40,640]{1,0:T(8,128)(2,1)S(1)}, u32[]{:S(2)}, u32[]{:S(2)}) collective-permute-start(bf16[40,640]{1,0:T(8,128)(2,1)S(1)} %shard_map.70), channel_id=1, source_target_pairs={{1,2},{2,1},{3,4},{4,3},{5,6},{6,5},{7,8},{8,7},{9,10},{10,9},{11,... | collective-permute-start | bytes 153608 | tf_op jit(solution)/shard_map/ppermute | solution.py:233
  12.8 15.8 %all-to-all-start = ((bf16[8,40,640]{2,1,0:T(8,128)(2,1)}), bf16[8,40,640]{2,1,0:T(8,128)(2,1)S(1)}, u32[]{:S(2)}, u32[]{:S(2)}) async-start(bf16[8,40,640]{2,1,0:T(8,128)(2,1)} %broadcast_in_dim.8), calls=%async_computation | async-start | bytes 819200 | tf_op jit(solution)/shard_map/all_to_all | solution.py:236
  19.3 12.0 %copy-start.1 = (s32[1,3]{1,0:T(1,128)S(1)}, s32[1,3]{1,0:T(1,128)}, u32[]{:S(2)}) copy-start(s32[1,3]{1,0:T(1,128)} %charge_ref.7) | copy-start | bytes 40
  19.3 9.3 %collective-permute-start = (bf16[320,640]{1,0:T(8,128)(2,1)S(1)}, bf16[320,640]{1,0:T(8,128)(2,1)S(1)}, u32[]{:S(2)}, u32[]{:S(2)}) collective-permute-start(bf16[320,640]{1,0:T(8,128)(2,1)S(1)} %shard_map.69), channel_id=1, source_target_pairs={{0,1},{1,0},{2,3},{3,2},{4,5},{5,4},{6,7},{7,6},{8,9},{9,8},{10,11... | collective-permute-start | bytes 1228808 | tf_op jit(solution)/shard_map/ppermute | solution.py:233
  28.6 2.6 %collective-permute-start.1 = (bf16[320,640]{1,0:T(8,128)(2,1)S(1)}, bf16[320,640]{1,0:T(8,128)(2,1)S(1)}, u32[]{:S(2)}, u32[]{:S(2)}) collective-permute-start(bf16[320,640]{1,0:T(8,128)(2,1)S(1)} %collective-permute-done.refs_1_), channel_id=1, source_target_pairs={{0,16},{1,17},{2,18},{3,19},{4,20},{5,21},{6,22},{7,23},{8,24},{9,... | collective-permute-start | bytes 1228808 | tf_op jit(solution)/shard_map/ppermute | solution.py:233
  28.6 2.6 %collective-permute-start.3 = (bf16[8,40,640]{2,1,0:T(8,128)(2,1)S(1)}, bf16[8,40,640]{2,1,0:T(8,128)(2,1)S(1)}, u32[]{:S(2)}, u32[]{:S(2)}) collective-permute-start(bf16[8,40,640]{2,1,0:T(8,128)(2,1)S(1)} %all-to-all-done.refs_4_), channel_id=1, source_target_pairs={{0,16},{1,17},{2,18},{3,19},{4,20},{5,21},{6,22},{7,23},{8,24},{9,... | collective-permute-start | bytes 1228808 | tf_op jit(solution)/shard_map/ppermute | solution.py:233
  34.9 3.1 %collective-permute-start.4 = (bf16[320,640]{1,0:T(8,128)(2,1)S(1)}, bf16[320,640]{1,0:T(8,128)(2,1)S(1)}, u32[]{:S(2)}, u32[]{:S(2)}) collective-permute-start(bf16[320,640]{1,0:T(8,128)(2,1)S(1)} %get-tuple-element.16), channel_id=1, source_target_pairs={{0,16},{1,17},{2,18},{3,19},{4,20},{5,21},{6,22},{7,23},{8,24},{9,... | collective-permute-start | bytes 1228808 | tf_op jit(solution)/shard_map/ppermute | solution.py:233
  53.6 10.2 %collective-permute-start.6 = (bf16[40,640]{1,0:T(8,128)(2,1)S(1)}, bf16[40,640]{1,0:T(8,128)(2,1)S(1)}, u32[]{:S(2)}, u32[]{:S(2)}) collective-permute-start(bf16[40,640]{1,0:T(8,128)(2,1)S(1)} %get-tuple-element.22), channel_id=1, source_target_pairs={{1,2},{2,1},{3,4},{4,3},{5,6},{6,5},{7,8},{8,7},{9,10},{10,9},{11,... | collective-permute-start | bytes 153608 | tf_op jit(solution)/shard_map/ppermute | solution.py:233
  58.6 5.2 %collective-permute-start.5 = (bf16[40,640]{1,0:T(8,128)(2,1)S(1)}, bf16[40,640]{1,0:T(8,128)(2,1)S(1)}, u32[]{:S(2)}, u32[]{:S(2)}) collective-permute-start(bf16[40,640]{1,0:T(8,128)(2,1)S(1)} %get-tuple-element.22), channel_id=1, source_target_pairs={{0,1},{1,0},{2,3},{3,2},{4,5},{5,4},{6,7},{7,6},{8,9},{9,8},{10,11... | collective-permute-start | bytes 153608 | tf_op jit(solution)/shard_map/ppermute | solution.py:233
  83.2 2.9 %collective-permute-start.7 = (bf16[8,3,40,640]{3,2,1,0:T(8,128)(2,1)S(1)}, bf16[8,3,40,640]{3,2,1,0:T(8,128)(2,1)S(1)}, u32[]{:S(2)}, u32[]{:S(2)}) collective-permute-start(bf16[8,3,40,640]{3,2,1,0:T(8,128)(2,1)S(1)} %all_to_all.21.refs_0_), channel_id=1, source_target_pairs={{0,16},{1,17},{2,18},{3,19},{4,20},{5,21},{6,22},{7,23},{8,24},{9,... | collective-permute-start | bytes 3686408 | tf_op jit(solution)/shard_map/ppermute | solution.py:233
  89.8 3.2 %collective-permute-start.8 = (bf16[320,640]{1,0:T(8,128)(2,1)S(1)}, bf16[320,640]{1,0:T(8,128)(2,1)S(1)}, u32[]{:S(2)}, u32[]{:S(2)}) collective-permute-start(bf16[320,640]{1,0:T(8,128)(2,1)S(1)} %get-tuple-element.20), channel_id=1, source_target_pairs={{0,16},{1,17},{2,18},{3,19},{4,20},{5,21},{6,22},{7,23},{8,24},{9,... | collective-permute-start | bytes 1228808 | tf_op jit(solution)/shard_map/ppermute | solution.py:233

commit v3 on v2

--- a/solution.py
+++ b/solution.py
@@ -15,6 +15,7 @@
 SMEM = pl.BlockSpec(memory_space=pltpu.SMEM)
 HBM = pl.BlockSpec(memory_space=pltpu.HBM)
 MIB = 2**20
+CHIP_ORDER = (0, 1, 3, 2, 4, 5, 7, 6)
 
 
 def swaps(ops_count, sec_count, partner):
@@ -78,7 +79,7 @@
             for block in range(blocks):
                 copies.append(
                     pltpu.make_async_copy(
-                        left_hbm.at[pair, pl.ds((2 * block + owner) * share, share), :],
+                        left_hbm.at[pair, pl.ds((2 * CHIP_ORDER[block] + owner) * share, share), :],
                         left_ref.at[pair, pl.ds((owner * blocks + block) * share, share), :],
                         sems.at[(pair * owners + owner) * blocks + block],
                     )
@@ -164,10 +165,10 @@
             for part, owner in ((near_ref, c), (far_ref, 1 - c)):
                 for block in range(blocks):
                     if n_whole:
-                        row = owner * half + block * share
+                        row = owner * half + CHIP_ORDER[block] * share
                         field_ref[2, row : row + share, :] = part[block]
                     else:
-                        row = (2 * block + owner) * share
+                        row = (2 * CHIP_ORDER[block] + owner) * share
                         for slot in range(3):
                             field_ref[slot, row : row + share, :] = part[block, slot]
 
@@ -227,7 +228,7 @@
     partner_core = swaps(ops_count, sec_count, lambda o, s: (o ^ 1, s))
     even = swaps(ops_count, sec_count, lambda o, s: (o, s ^ 1))
     odd = swaps(ops_count, sec_count, lambda o, s: (o, s + 1 if s % 2 else s - 1))
-    same_core = [[o for o in range(ops_count) if o % 2 == c] for c in range(2)]
+    same_core = [[2 * chip + c for chip in CHIP_ORDER] for c in range(2)]
 
     def send(block, where):
         return lax.ppermute(block, AXES, where)
@@ -259,16 +260,23 @@
         partner_sum = send(other, partner_core)
         mine = mine_rows(charge_step, field, left, right)
         chip_sum = (mine + partner_sum.astype(jnp.float32)).astype(jnp.bfloat16)
-        applied = exchange(chip_sum.reshape(chips, share, width)).astype(jnp.float32).sum(axis=0) * scaled_mask
-        updated = applied if iteration == 0 else 2.0 * applied - outputs[-2]
-        outputs.append(updated)
+        summed = exchange(chip_sum.reshape(chips, share, width)).astype(jnp.float32).sum(axis=0)
+
+        def updated(total):
+            applied = total * scaled_mask
+            return applied if iteration == 0 else 2.0 * applied - outputs[iteration - 1]
+
         if iteration + 1 < STEPS:
-            rows = updated.astype(jnp.bfloat16)
-            even_rows = send(rows, even)
-            three = jnp.stack([rows, even_rows, send(rows, odd)])
+            rows = updated(summed).astype(jnp.bfloat16)
+            even_rows, odd_rows = send(rows, even), send(rows, odd)
+            later, odd_rows = lax.optimization_barrier((summed, odd_rows))
+            outputs.append(updated(later))
+            three = jnp.stack([rows, even_rows, odd_rows])
             near = spread(three)
             far = send(near, partner_core)
             wholes = []
+        else:
+            outputs.append(updated(summed))
     return (outputs[-2][None], outputs[-1][None])
 
 

time: 107 us -> 106 us (level)
  no operation moved by 1% of the time
where the time goes in v3:
time: 106 us; the launch traced here: 105 us
  blocking collectives  45.4 us (43%)
  waiting for transfers between devices  23.7 us (22%)
  Pallas kernels  17.6 us (17%)
  starting transfers between devices  15.2 us (14%)
    all_to_all x3, blocking collectives, exchange(): lax.all_to_all(tiles, 'ops', 0, 0, axis_index_groups=same_core, tiled=True)  45.4 us
    ppermute x9, waiting for transfers between devices, send(): return lax.ppermute(block, AXES, where)  23.7 us
    ppermute x9, starting transfers between devices, send(): return lax.ppermute(block, AXES, where)  10 us
    pallas_call x2, Pallas kernels, other_rows(): pl.pallas_call(functools.partial(other_kernel, len(wholes)), in_specs=[SM...  7.24 us
    pallas_call x2, Pallas kernels, mine_rows(): pl.pallas_call(mine_kernel, in_specs=[SMEM, VMEM, VMEM, VMEM], out_specs=...  5.94 us
    all_to_all x1, starting transfers between devices, exchange(): lax.all_to_all(tiles, 'ops', 0, 0, axis_index_groups=same_core, tiled=True)  5.2 us
    pallas_call x2, Pallas kernels, masked_rows(): pl.pallas_call(functools.partial(cut_kernel, first_row), in_specs=[HBM, H...  2.32 us
  transfers between devices with their start and end apart: 10, of which 4 were waited for; matrix products, arithmetic and copies ran while one was open for 0% of the time, Pallas kernels for 9%

profile of v3, /device:TPU:128, one launch (start us, length us, event | category | flops | bytes accessed | tf_op | source)
XLA Modules:
  0.0 104.7 jit_solution(14636871494792993260)
XLA Ops:
  0.6 1.1 %shard_map.70 = bf16[40,640]{1,0:T(8,128)(2,1)S(1)} custom-call(s32[16]{0:T(128)} %sizes_ref.5, f32[640,640]{1,0:T(8,128)} %bitcast.17), custom_call_target="tpu_custom_call" | custom-call | flops 25600 | bytes 153600 | tf_op jit(solution)/shard_map/pallas_call | solution.py:58
  1.7 4.0 %collective-permute-start.2 = (bf16[40,640]{1,0:T(8,128)(2,1)S(1)}, bf16[40,640]{1,0:T(8,128)(2,1)S(1)}, u32[]{:S(2)}, u32[]{:S(2)}) collective-permute-start(bf16[40,640]{1,0:T(8,128)(2,1)S(1)} %shard_map.70), channel_id=1, source_target_pairs={{1,2},{2,1},{3,4},{4,3},{5,6},{6,5},{7,8},{8,7},{9,10},{10,9},{11,... | collective-permute-start | bytes 153608 | tf_op jit(solution)/shard_map/ppermute | solution.py:234
  5.7 6.3 %collective-permute-done.2 = bf16[40,640]{1,0:T(8,128)(2,1)S(1)} collective-permute-done((bf16[40,640]{1,0:T(8,128)(2,1)S(1)}, bf16[40,640]{1,0:T(8,128)(2,1)S(1)}, u32[]{:S(2)}, u32[]{:S(2)}) %collective-permute-start.2) | collective-permute-done | bytes 51232 | tf_op jit(solution)/shard_map/ppermute | solution.py:234
  12.0 0.8 broadcast_in_dim.8
  12.8 5.2 %all-to-all-start = ((bf16[8,40,640]{2,1,0:T(8,128)(2,1)}), bf16[8,40,640]{2,1,0:T(8,128)(2,1)S(1)}, u32[]{:S(2)}, u32[]{:S(2)}) async-start(bf16[8,40,640]{2,1,0:T(8,128)(2,1)} %broadcast_in_dim.8), calls=%async_computation | async-start | bytes 819200 | tf_op jit(solution)/shard_map/all_to_all | solution.py:237
  18.0 1.3 %shard_map.69 = bf16[320,640]{1,0:T(8,128)(2,1)S(1)} custom-call(s32[16]{0:T(128)} %sizes_ref.5, f32[640,640]{1,0:T(8,128)} %bitcast.18), custom_call_target="tpu_custom_call" | custom-call | flops 204800 | bytes 1228800 | tf_op jit(solution)/shard_map/pallas_call | solution.py:58
  19.4 9.2 %collective-permute-done.refs_1_ = bf16[320,640]{1,0:T(8,128)(2,1)S(1)} collective-permute-done((bf16[320,640]{1,0:T(8,128)(2,1)S(1)}, bf16[320,640]{1,0:T(8,128)(2,1)S(1)}, u32[]{:S(2)}, u32[]{:S(2)}) %collective-permute-start) | collective-permute-done | bytes 409632 | tf_op jit(solution)/shard_map/ppermute | solution.py:234
  28.6 0.5 collective-permute-start.3
  29.2 2.1 %shard_map.68 = (bf16[640,640]{1,0:T(8,128)(2,1)S(1)}, f32[40,640]{1,0:T(8,128)S(1)}, f32[40,640]{1,0:T(8,128)S(1)}, bf16[3,640,640]{2,1,0:T(8,128)(2,1)S(1)}) custom-call(s32[16]{0:T(128)} %sizes_ref.5, f32[640,640]{1,0:T(8,128)S(1)} %bitcast.19, bf16[3,640,640]{2,1,0:T(8,128)(2,1)} %bitcast.22), custom_call_target="tpu_custom_call" | custom-call | flops 409600 | bytes 7372800 | tf_op jit(solution)/shard_map/pallas_call | solution.py:103
  31.3 3.6 %shard_map.71 = (bf16[320,640]{1,0:T(8,128)(2,1)S(1)}, bf16[3,640,640]{2,1,0:T(8,128)(2,1)S(1)}, bf16[3,640,640]{2,1,0:T(8,128)(2,1)S(1)}) custom-call(s32[1,3]{1,0:T(1,128)S(1)} %copy-done.1, bf16[640,640]{1,0:T(8,128)(2,1)S(1)} %get-tuple-element.14.refs_0_, bf16[320,640]{1,0:T(8,128)(2,1)S(1)} %collective-permute-done.refs_1_, ...), custom_call_target="tpu_custom_call" | custom-call | flops 1572864000 | bytes 4915200 | tf_op jit(solution)/shard_map/pallas_call | solution.py:191
  34.9 0.1 collective-permute-start.4
  35.0 3.0 %shard_map.72 = f32[320,640]{1,0:T(8,128)S(1)} custom-call(s32[1,3]{1,0:T(1,128)S(1)} %copy-done.1, bf16[3,640,640]{2,1,0:T(8,128)(2,1)S(1)} %get-tuple-element.16.field_ref, bf16[3,640,640]{2,1,0:T(8,128)(2,1)S(1)} %get-tuple-element.15.refs_6_.left_ref.refs_2_, bf16[3,640,640]{2,1,0:T(8,128)(2,1)S(1)} %get-tuple-element.17.right_ref), custom_call_target="tpu_custom_call" | custom-call | flops 1572864000 | bytes 4915200 | tf_op jit(solution)/shard_map/pallas_call | solution.py:211
  38.1 14.6 %all_to_all.20 = bf16[8,40,640]{2,1,0:T(8,128)(2,1)S(1)} all-to-all(bf16[8,40,640]{2,1,0:T(8,128)(2,1)S(1)} %bitcast.23), channel_id=1, replica_groups={{0,32,96,64,128,160,224,192},{16,48,112,80,144,176,240,208},{1,33,97,65..., dimensions={0} | all-to-all | bytes 819200 | tf_op jit(solution)/shard_map/all_to_all | solution.py:237
  52.8 5.0 %collective-permute-start.5 = (bf16[40,640]{1,0:T(8,128)(2,1)S(1)}, bf16[40,640]{1,0:T(8,128)(2,1)S(1)}, u32[]{:S(2)}, u32[]{:S(2)}) collective-permute-start(bf16[40,640]{1,0:T(8,128)(2,1)S(1)} %multiply_convert_fusion), channel_id=1, source_target_pairs={{1,2},{2,1},{3,4},{4,3},{5,6},{6,5},{7,8},{8,7},{9,10},{10,9},{11,... | collective-permute-start | bytes 153608 | tf_op jit(solution)/shard_map/ppermute | solution.py:234
  57.9 5.2 %collective-permute-done.5 = bf16[40,640]{1,0:T(8,128)(2,1)S(1)} collective-permute-done((bf16[40,640]{1,0:T(8,128)(2,1)S(1)}, bf16[40,640]{1,0:T(8,128)(2,1)S(1)}, u32[]{:S(2)}, u32[]{:S(2)}) %collective-permute-start.5) | collective-permute-done | bytes 51232 | tf_op jit(solution)/shard_map/ppermute | solution.py:234
  63.1 0.1 broadcast_in_dim.20
  63.2 18.8 %all_to_all.21.refs_0_ = bf16[8,3,40,640]{3,2,1,0:T(8,128)(2,1)S(1)} all-to-all(bf16[8,3,40,640]{3,2,1,0:T(8,128)(2,1)S(1)} %broadcast_in_dim.20), channel_id=1, replica_groups={{0,32,96,64,128,160,224,192},{16,48,112,80,144,176,240,208},{1,33,97,65..., dimensions={0} | all-to-all | bytes 2457600 | tf_op jit(solution)/shard_map/all_to_all | solution.py:237
  82.0 2.9 %collective-permute-done.7.refs_1_ = bf16[8,3,40,640]{3,2,1,0:T(8,128)(2,1)S(1)} collective-permute-done((bf16[8,3,40,640]{3,2,1,0:T(8,128)(2,1)S(1)}, bf16[8,3,40,640]{3,2,1,0:T(8,128)(2,1)S(1)}, u32[]{:S(2)}, u32[]{:S(2)}) %collective-permute-start.7) | collective-permute-done | bytes 1228832 | tf_op jit(solution)/shard_map/ppermute | solution.py:234
  85.0 3.6 %shard_map.73 = (bf16[320,640]{1,0:T(8,128)(2,1)S(1)}, bf16[3,640,640]{2,1,0:T(8,128)(2,1)S(1)}, bf16[3,640,640]{2,1,0:T(8,128)(2,1)S(1)}) custom-call(s32[1,3]{1,0:T(1,128)S(1)} %copy-done.1, bf16[8,3,40,640]{3,2,1,0:T(8,128)(2,1)S(1)} %all_to_all.21.refs_0_, bf16[8,3,40,640]{3,2,1,0:T(8,128)(2,1)S(1)} %collective-permute-done.7.refs_1_, ...), custom_call_target="tpu_custom_call" | custom-call | flops 1572864000 | bytes 4915200 | tf_op jit(solution)/shard_map/pallas_call | solution.py:191
  88.6 0.2 collective-permute-start.8
  88.8 3.0 %shard_map.74 = f32[320,640]{1,0:T(8,128)S(1)} custom-call(s32[1,3]{1,0:T(1,128)S(1)} %copy-done.1, bf16[3,640,640]{2,1,0:T(8,128)(2,1)S(1)} %get-tuple-element.22.field_ref, bf16[3,640,640]{2,1,0:T(8,128)(2,1)S(1)} %get-tuple-element.15.refs_6_.left_ref.refs_2_, bf16[3,640,640]{2,1,0:T(8,128)(2,1)S(1)} %get-tuple-element.23.right_ref), custom_call_target="tpu_custom_call" | custom-call | flops 1572864000 | bytes 4915200 | tf_op jit(solution)/shard_map/pallas_call | solution.py:211
  91.8 0.1 add_convert_fusion
  91.9 12.0 %all_to_all.22 = bf16[8,40,640]{2,1,0:T(8,128)(2,1)S(1)} all-to-all(bf16[8,40,640]{2,1,0:T(8,128)(2,1)S(1)} %bitcast.24), channel_id=1, replica_groups={{0,32,96,64,128,160,224,192},{16,48,112,80,144,176,240,208},{1,33,97,65..., dimensions={0} | all-to-all | bytes 819200 | tf_op jit(solution)/shard_map/all_to_all | solution.py:237
  104.0 0.7 subtract_bitcast_fusion
  (20 shorter events, 0.5 us)
Async XLA Ops:
  0.6 28.5 %copy-start = (f32[1,640,640]{2,1,0:T(8,128)S(1)}, f32[1,640,640]{2,1,0:T(8,128)}, u32[]{:S(2)}) copy-start(f32[1,640,640]{2,1,0:T(8,128)} %param.5) | copy-start | bytes 4915204
  1.7 10.3 %collective-permute-start.2 = (bf16[40,640]{1,0:T(8,128)(2,1)S(1)}, bf16[40,640]{1,0:T(8,128)(2,1)S(1)}, u32[]{:S(2)}, u32[]{:S(2)}) collective-permute-start(bf16[40,640]{1,0:T(8,128)(2,1)S(1)} %shard_map.70), channel_id=1, source_target_pairs={{1,2},{2,1},{3,4},{4,3},{5,6},{6,5},{7,8},{8,7},{9,10},{10,9},{11,... | collective-permute-start | bytes 153608 | tf_op jit(solution)/shard_map/ppermute | solution.py:234
  12.8 15.8 %all-to-all-start = ((bf16[8,40,640]{2,1,0:T(8,128)(2,1)}), bf16[8,40,640]{2,1,0:T(8,128)(2,1)S(1)}, u32[]{:S(2)}, u32[]{:S(2)}) async-start(bf16[8,40,640]{2,1,0:T(8,128)(2,1)} %broadcast_in_dim.8), calls=%async_computation | async-start | bytes 819200 | tf_op jit(solution)/shard_map/all_to_all | solution.py:237
  19.3 12.0 %copy-start.1 = (s32[1,3]{1,0:T(1,128)S(1)}, s32[1,3]{1,0:T(1,128)}, u32[]{:S(2)}) copy-start(s32[1,3]{1,0:T(1,128)} %charge_ref.7) | copy-start | bytes 40
  19.3 9.3 %collective-permute-start = (bf16[320,640]{1,0:T(8,128)(2,1)S(1)}, bf16[320,640]{1,0:T(8,128)(2,1)S(1)}, u32[]{:S(2)}, u32[]{:S(2)}) collective-permute-start(bf16[320,640]{1,0:T(8,128)(2,1)S(1)} %shard_map.69), channel_id=1, source_target_pairs={{0,1},{1,0},{2,3},{3,2},{4,5},{5,4},{6,7},{7,6},{8,9},{9,8},{10,11... | collective-permute-start | bytes 1228808 | tf_op jit(solution)/shard_map/ppermute | solution.py:234
  28.6 2.6 %collective-permute-start.1 = (bf16[320,640]{1,0:T(8,128)(2,1)S(1)}, bf16[320,640]{1,0:T(8,128)(2,1)S(1)}, u32[]{:S(2)}, u32[]{:S(2)}) collective-permute-start(bf16[320,640]{1,0:T(8,128)(2,1)S(1)} %collective-permute-done.refs_1_), channel_id=1, source_target_pairs={{0,16},{1,17},{2,18},{3,19},{4,20},{5,21},{6,22},{7,23},{8,24},{9,... | collective-permute-start | bytes 1228808 | tf_op jit(solution)/shard_map/ppermute | solution.py:234
  28.6 2.6 %collective-permute-start.3 = (bf16[8,40,640]{2,1,0:T(8,128)(2,1)S(1)}, bf16[8,40,640]{2,1,0:T(8,128)(2,1)S(1)}, u32[]{:S(2)}, u32[]{:S(2)}) collective-permute-start(bf16[8,40,640]{2,1,0:T(8,128)(2,1)S(1)} %all-to-all-done.refs_4_), channel_id=1, source_target_pairs={{0,16},{1,17},{2,18},{3,19},{4,20},{5,21},{6,22},{7,23},{8,24},{9,... | collective-permute-start | bytes 1228808 | tf_op jit(solution)/shard_map/ppermute | solution.py:234
  34.9 3.1 %collective-permute-start.4 = (bf16[320,640]{1,0:T(8,128)(2,1)S(1)}, bf16[320,640]{1,0:T(8,128)(2,1)S(1)}, u32[]{:S(2)}, u32[]{:S(2)}) collective-permute-start(bf16[320,640]{1,0:T(8,128)(2,1)S(1)} %get-tuple-element.18), channel_id=1, source_target_pairs={{0,16},{1,17},{2,18},{3,19},{4,20},{5,21},{6,22},{7,23},{8,24},{9,... | collective-permute-start | bytes 1228808 | tf_op jit(solution)/shard_map/ppermute | solution.py:234
  52.8 10.3 %collective-permute-start.5 = (bf16[40,640]{1,0:T(8,128)(2,1)S(1)}, bf16[40,640]{1,0:T(8,128)(2,1)S(1)}, u32[]{:S(2)}, u32[]{:S(2)}) collective-permute-start(bf16[40,640]{1,0:T(8,128)(2,1)S(1)} %multiply_convert_fusion), channel_id=1, source_target_pairs={{1,2},{2,1},{3,4},{4,3},{5,6},{6,5},{7,8},{8,7},{9,10},{10,9},{11,... | collective-permute-start | bytes 153608 | tf_op jit(solution)/shard_map/ppermute | solution.py:234
  57.8 5.3 %collective-permute-start.6 = (bf16[40,640]{1,0:T(8,128)(2,1)S(1)}, bf16[40,640]{1,0:T(8,128)(2,1)S(1)}, u32[]{:S(2)}, u32[]{:S(2)}) collective-permute-start(bf16[40,640]{1,0:T(8,128)(2,1)S(1)} %multiply_convert_fusion), channel_id=1, source_target_pairs={{0,1},{1,0},{2,3},{3,2},{4,5},{5,4},{6,7},{7,6},{8,9},{9,8},{10,11... | collective-permute-start | bytes 153608 | tf_op jit(solution)/shard_map/ppermute | solution.py:234
  82.0 2.9 %collective-permute-start.7 = (bf16[8,3,40,640]{3,2,1,0:T(8,128)(2,1)S(1)}, bf16[8,3,40,640]{3,2,1,0:T(8,128)(2,1)S(1)}, u32[]{:S(2)}, u32[]{:S(2)}) collective-permute-start(bf16[8,3,40,640]{3,2,1,0:T(8,128)(2,1)S(1)} %all_to_all.21.refs_0_), channel_id=1, source_target_pairs={{0,16},{1,17},{2,18},{3,19},{4,20},{5,21},{6,22},{7,23},{8,24},{9,... | collective-permute-start | bytes 3686408 | tf_op jit(solution)/shard_map/ppermute | solution.py:234
  88.6 3.2 %collective-permute-start.8 = (bf16[320,640]{1,0:T(8,128)(2,1)S(1)}, bf16[320,640]{1,0:T(8,128)(2,1)S(1)}, u32[]{:S(2)}, u32[]{:S(2)}) collective-permute-start(bf16[320,640]{1,0:T(8,128)(2,1)S(1)} %get-tuple-element.24), channel_id=1, source_target_pairs={{0,16},{1,17},{2,18},{3,19},{4,20},{5,21},{6,22},{7,23},{8,24},{9,... | collective-permute-start | bytes 1228808 | tf_op jit(solution)/shard_map/ppermute | solution.py:234
